TPU v7x, 32 devices: a whole 2x2x4 slice. The times are simulated.
32 devices in a mesh: blk: 8 (over z, y), chan: 4 (over x, core).
Axes of the slice: x: 2, y: 2, z: 4, core: 2. Of those that a mesh axis runs over, the one named last changes fastest.
Arguments:
- hidden_in: bfloat16 [2, 1, 2048, 768], P(None, None, ('blk', 'chan')), may hold values from -6 to 6
- cotangent: bfloat16 [2, 1, 2048, 768], P(None, None, ('blk', 'chan')), may hold values from -6 to 6
- mixer_input_weight: bfloat16 [768, 2304], P(None, ('blk', 'chan')), may hold values from -0.21875 to 0.21875
- mixer_output_weight: bfloat16 [768, 768], P(None, ('blk', 'chan')), may hold values from -0.21875 to 0.21875
- feedforward_up: bfloat16 [768, 3072], P(None, ('blk', 'chan')), may hold values from -0.21875 to 0.21875
- feedforward_down: bfloat16 [3072, 768], P(('blk', 'chan')), may hold values from -0.109375 to 0.109375
- first_gain: bfloat16 [768], P(('blk', 'chan')), may hold values from 0.5 to 1.5
- first_shift: bfloat16 [768], P(('blk', 'chan')), may hold values from -3 to 3
- second_gain: bfloat16 [768], P(('blk', 'chan')), may hold values from 0.5 to 1.5
- second_shift: bfloat16 [768], P(('blk', 'chan')), may hold values from -3 to 3
- short_taps: bfloat16 [3, 3, 768], P(None, None, ('blk', 'chan')), may hold values from -4 to 4
- short_bias: bfloat16 [3, 768], P(None, ('blk', 'chan')), may hold values from -3 to 3
- skip_scale: bfloat16 [768], P(('blk', 'chan')), may hold values from -4 to 4
- filter_out: bfloat16 [64, 768], P(None, ('blk', 'chan')), may hold values from -0.023925781 to 0.023925781
- pos_weight: bfloat16 [33, 64], replicated, may hold values from -1 to 1
- pos_bias: bfloat16 [64], replicated, may hold values from -4 to 4
- mid_weight: bfloat16 [64, 64], replicated, may hold values from -0.75 to 0.75
- mid_bias: bfloat16 [64], replicated, may hold values from -4 to 4
- sine_freq: bfloat16 [64], replicated, may hold values from 2 to 16
- decay_rate: bfloat16 [768], P(('blk', 'chan')), may hold values from 0.00024414062 to 0.029907227
Outputs:
- hidden_out: bfloat16 [2, 1, 2048, 768], P(None, None, ('blk', 'chan'))
- grad_hidden: bfloat16 [2, 1, 2048, 768], P(None, None, ('blk', 'chan'))
- grad_mixer_in: float32 [768, 2304], P(None, ('blk', 'chan'))
- grad_mixer_out: float32 [768, 768], P(None, ('blk', 'chan'))
- grad_mlp_up: float32 [768, 3072], P(None, ('blk', 'chan'))
- grad_mlp_down: float32 [3072, 768], P(('blk', 'chan'))
- grad_first_gain: float32 [768], P(('blk', 'chan'))
- grad_first_shift: float32 [768], P(('blk', 'chan'))
- grad_second_gain: float32 [768], P(('blk', 'chan'))
- grad_second_shift: float32 [768], P(('blk', 'chan'))
- grad_short_taps: float32 [3, 3, 768], P(None, None, ('blk', 'chan'))
- grad_short_bias: float32 [3, 768], P(None, ('blk', 'chan'))
- grad_skip_scale: float32 [768], P(('blk', 'chan'))
- grad_filter_out: float32 [64, 768], P(None, ('blk', 'chan'))
- grad_pos_weight: float32 [33, 64], replicated
- grad_pos_bias: float32 [64], replicated
- grad_mid_weight: float32 [64, 64], replicated
- grad_mid_bias: float32 [64], replicated
- grad_sine_freq: float32 [64], replicated
All inputs are finite; a program needn't handle non-finite values.
Results may differ from a plain program's by a relative error of at most 0.012.
Values may be sent and summed in bfloat16 or wider, within the bound.
A program may use at most 320 MiB of HBM per device.

v0:
```python
import functools
import math

import jax
import jax.numpy as jnp
import numpy as np
from jax import lax
from jax.experimental import pallas as pl
from jax.experimental.pallas import tpu as pltpu
from jax.sharding import PartitionSpec as P

EPS = 1e-05
BANDS = 16
EXACT = lax.Precision.HIGHEST
AXES = ("blk", "chan")
F32 = jnp.float32
BF16 = jnp.bfloat16
MESH = pl.DeviceIdType.MESH
KERNEL_VMEM = 62 << 20


def contract(a, b, dim_a, dim_b, precision=None):
    return lax.dot_general(
        a, b, (((dim_a,), (dim_b,)), ((), ())), precision=precision, preferred_element_type=F32
    )


def positions(length):
    lags = jnp.arange(length).astype(F32)
    band_freq = 0.0001 + (BANDS - 1 - 0.0001) * jnp.arange(BANDS).astype(F32) / (BANDS - 1)
    phase = 2.0 * math.pi / length * lags[None, :] * band_freq[:, None]
    return lags, jnp.concatenate([lags[None, :] / (length - 1), jnp.cos(phase), -jnp.sin(phase)], 0)


def feature_blocks(length, block):
    lags = np.arange(length).astype(np.float32)
    bands = np.arange(BANDS).astype(np.float32)
    band_freq = np.float32(0.0001) + np.float32(BANDS - 1 - 0.0001) * bands / np.float32(BANDS - 1)
    phase = np.float32(2.0 * math.pi / length) * lags[None, :] * band_freq[:, None]
    ramp = lags[None, :] / np.float32(length - 1)
    rows = np.concatenate([ramp, np.cos(phase), -np.sin(phase), np.ones_like(ramp)])
    rows = np.pad(rows, ((0, -len(rows) % 8), (0, 0))).astype(np.float32)
    return np.ascontiguousarray(rows.reshape(len(rows), -1, block).transpose(1, 0, 2))


def fixed_table(block):
    spot, freq = np.arange(block)[:, None], np.arange(block)[None, :]
    phase = (np.pi / block) * (spot * freq % (2 * block))
    imag = np.where(freq == 0, 1.0 - 2.0 * (spot % 2), -np.sin(phase))
    return np.concatenate([np.cos(phase), imag], 1).astype(np.float32)


def filter_hidden(length, pos_weight, pos_bias, mid_weight, mid_bias, sine_freq):
    lags, features = positions(length)
    freq = sine_freq[:, None]
    first_sum = contract(pos_weight, features, 0, 0, EXACT) + pos_bias[:, None]
    first = jnp.sin(freq * first_sum)
    second_sum = contract(mid_weight, first, 0, 0, EXACT) + mid_bias[:, None]
    second = jnp.sin(freq * second_sum)
    return lags, features, first_sum, first, second_sum, second


def block_table(block):
    spot = lax.broadcasted_iota(jnp.int32, (block, block), 0)
    freq = lax.broadcasted_iota(jnp.int32, (block, block), 1)
    phase = (math.pi / block) * (spot * freq % (2 * block)).astype(F32)
    parity = 1.0 - 2.0 * (spot % 2).astype(F32)
    imag = jnp.where(freq == 0, parity, -jnp.sin(phase))
    return jnp.concatenate([jnp.cos(phase), imag], 1)


def to_spectrum(blocks, table):
    spec = lax.dot_general(
        blocks, table, (((blocks.ndim - 1,), (0,)), ((), ())), precision=EXACT, preferred_element_type=F32
    )
    half = table.shape[0]
    return spec[..., :half], spec[..., half:]


def from_spectrum(real, imag, table):
    half = table.shape[0]
    weight = jnp.where(lax.iota(jnp.int32, half) == 0, 0.5 / half, 1.0 / half)
    spec = jnp.concatenate([real * weight, imag * weight], -1)
    return lax.dot_general(
        spec, table, (((spec.ndim - 1,), (1,)), ((), ())), precision=EXACT, preferred_element_type=F32
    )


def packed_kernel(real, imag):
    first = lax.iota(jnp.int32, real.shape[-1]) == 0
    return real, jnp.where(first, imag, real), jnp.where(first, 0.0, imag)


def layer_norm(values, gain, shift):
    center = values - jnp.mean(values, -1, keepdims=True)
    scale_inv = lax.rsqrt(jnp.mean(center * center, -1, keepdims=True) + EPS)
    normal = center * scale_inv
    return normal * gain + shift, normal, scale_inv


def layer_norm_back(grad_out, normal, scale_inv, gain):
    grad_normal = grad_out * gain
    inner = grad_normal - jnp.mean(grad_normal, -1, keepdims=True)
    inner = inner - normal * jnp.mean(grad_normal * normal, -1, keepdims=True)
    return inner * scale_inv, jnp.sum(grad_out * normal, 0), jnp.sum(grad_out, 0)


def gelu_parts(v):
    root = math.sqrt(2.0 / math.pi)
    inner = root * (v + 0.044715 * v * v * v)
    t = jnp.tanh(inner)
    value = 0.5 * v * (1.0 + t)
    slope = 0.5 * (1.0 + t) + 0.5 * v * (1.0 - t * t) * root * (1.0 + 3.0 * 0.044715 * v * v)
    return value, slope


def delayed(values, steps):
    if steps == 0:
        return values
    pad = jnp.zeros(values.shape[:-1] + (steps,), values.dtype)
    return jnp.concatenate([pad, values[..., :-steps]], -1)


def advanced(values, steps):
    if steps == 0:
        return values
    pad = jnp.zeros(values.shape[:-1] + (steps,), values.dtype)
    return jnp.concatenate([values[..., steps:], pad], -1)


def exchange(values):
    return lax.all_to_all(values, AXES, split_axis=0, concat_axis=0, tiled=True)


def spot():
    b, c = lax.axis_index("blk"), lax.axis_index("chan")
    return b // 2, b % 2, c // 2, c % 2


def at(z, y, x, k):
    return {"blk": z * 2 + y, "chan": x * 2 + k}


def flat(z, y, x, k):
    return ((z * 2 + y) * 2 + x) * 2 + k


def when(condition, act):
    pl.when(condition)(act)


def send(src, dst, send_sem, recv_sem, place):
    return pltpu.make_async_remote_copy(
        src_ref=src, dst_ref=dst, send_sem=send_sem, recv_sem=recv_sem, device_id=at(*place), device_id_type=MESH
    )


def greet_all(count):
    b, c = lax.axis_index("blk"), lax.axis_index("chan")
    chan = lax.axis_size("chan")
    me = b * chan + c
    barrier = pltpu.get_barrier_semaphore()

    def one(i, carry):
        other = lax.rem(me + i, count)
        pl.semaphore_signal(
            barrier, inc=1, device_id={"blk": other // chan, "chan": other % chan}, device_id_type=MESH
        )
        return carry

    lax.fori_loop(1, count, one, 0)
    pl.semaphore_wait(barrier, count - 1)


def greet_near(line):
    z, y, x, k = spot()
    barrier = pltpu.get_barrier_semaphore()

    def hello(*place):
        pl.semaphore_signal(barrier, inc=1, device_id=at(*place), device_id_type=MESH)

    hello(z, 1 - y, x, k)
    hello(z, y, 1 - x, k)
    hello(z, y, x, 1 - k)
    when(z > 0, lambda: hello(z - 1, y, x, k))
    when(z < line - 1, lambda: hello(z + 1, y, x, k))
    pl.semaphore_wait(barrier, 3 + jnp.minimum(z, 1) + jnp.minimum(line - 1 - z, 1))


def low_rows(rows):
    return max(rows // 16 * 8, 8) if rows > 8 else rows


class Gather:
    def __init__(self, line, shard, full, sends, recvs, local):
        self.line, self.shard, self.full, self.s, self.r, self.local = line, shard, full, sends, recvs, local
        self.rows = shard.shape[0]
        self.low = low_rows(self.rows)
        self.z, self.y, self.x, self.k = spot()

    def copy(self, kind, index, shard, place, rows=None):
        ref = self.full.at[shard] if rows is None else self.full.at[shard, pl.ds(*rows)]
        return send(ref, ref, self.s.at[kind, index], self.r.at[kind, index], place)

    def up(self, zo):
        return self.copy(0, zo, flat(zo, self.y, self.x, self.k), (self.z + 1, self.y, self.x, self.k))

    def down(self, zo):
        return self.copy(1, zo, flat(zo, self.y, self.x, self.k), (self.z - 1, self.y, self.x, self.k))

    def to_x(self, zo):
        return self.copy(2, zo, flat(zo, self.y, self.x, self.k), (self.z, self.y, 1 - self.x, self.k))

    def to_y(self, zo):
        return self.copy(3, zo, flat(zo, self.y, self.x, self.k), (self.z, 1 - self.y, self.x, self.k))

    def low_y(self, zo, other_y=False):
        shard = flat(zo, 1 - self.y if other_y else self.y, 1 - self.x, self.k)
        return self.copy(4, zo, shard, (self.z, 1 - self.y, self.x, self.k), (0, self.low))

    def high_x(self, zo, other_x=False):
        shard = flat(zo, 1 - self.y, 1 - self.x if other_x else self.x, self.k)
        return self.copy(5, zo, shard, (self.z, self.y, 1 - self.x, self.k), (self.low, self.rows - self.low))

    def core(self, zo, yo, xo, k):
        return self.copy(6, (zo * 2 + yo) * 2 + xo, flat(zo, yo, xo, k), (self.z, self.y, self.x, 1 - self.k))

    def line_has(self, zo):
        self.to_x(zo).start()
        self.to_y(zo).start()
        self.core(zo, self.y, self.x, self.k).start()

    def begin(self):
        own = self.full.at[flat(self.z, self.y, self.x, self.k)]
        copy = pltpu.make_async_copy(self.shard, own, self.local)
        copy.start()
        copy.wait()
        when(self.z < self.line - 1, lambda: self.up(self.z).start())
        when(self.z > 0, lambda: self.down(self.z).start())
        self.line_has(self.z)

    def each(self, distance, act):
        if distance == 0:
            act(self.z)
        else:
            when(self.z - distance >= 0, lambda: act(self.z - distance))
            when(self.z + distance < self.line, lambda: act(self.z + distance))

    def along(self, distance):
        def from_below():
            zo = self.z - distance
            self.up(zo).wait_recv()
            when(self.z < self.line - 1, lambda: self.up(zo).start())
            self.line_has(zo)

        def from_above():
            zo = self.z + distance
            self.down(zo).wait_recv()
            when(self.z > 0, lambda: self.down(zo).start())
            self.line_has(zo)

        when(self.z - distance >= 0, from_below)
        when(self.z + distance < self.line, from_above)

    def plane(self, distance):
        def act(zo):
            self.to_x(zo).wait_recv()
            self.low_y(zo).start()
            self.core(zo, self.y, 1 - self.x, self.k).start()
            self.to_y(zo).wait_recv()
            if self.low < self.rows:
                self.high_x(zo).start()
            self.core(zo, 1 - self.y, self.x, self.k).start()

        self.each(distance, act)

    def corner(self, distance):
        def act(zo):
            self.low_y(zo, True).wait_recv()
            if self.low < self.rows:
                self.high_x(zo, True).wait_recv()
            self.core(zo, 1 - self.y, 1 - self.x, self.k).start()

        self.each(distance, act)

    def finish(self):
        for zo in range(self.line):
            for yo in range(2):
                for xo in range(2):
                    self.core(zo, yo, xo, 1 - self.k).wait_recv()

    def drain(self):
        for zo in range(self.line):
            when(jnp.logical_and(self.z < self.line - 1, zo <= self.z), lambda: self.up(zo).wait_send())
            when(jnp.logical_and(self.z > 0, zo >= self.z), lambda: self.down(zo).wait_send())
            self.to_x(zo).wait_send()
            self.to_y(zo).wait_send()
            self.low_y(zo).wait_send()
            if self.low < self.rows:
                self.high_x(zo).wait_send()
            for yo in range(2):
                for xo in range(2):
                    self.core(zo, yo, xo, self.k).wait_send()


class Reduce:
    def __init__(self, line, part, out, chip, low_y, high_x, by_x, by_y, by_z, sends, recvs):
        self.line, self.part, self.out, self.chip = line, part, out, chip
        self.low_buf, self.high_buf, self.x_buf, self.y_buf, self.z_buf = low_y, high_x, by_x, by_y, by_z
        self.s, self.r = sends, recvs
        self.rows = part.shape[1]
        self.low = low_rows(self.rows)
        self.z, self.y, self.x, self.k = spot()

    def index(self, zo, yo, xo):
        return (zo * 2 + yo) * 2 + xo

    def copy(self, kind, index, src, dst, place):
        return send(src, dst, self.s.at[kind, index], self.r.at[kind, index], place)

    def core(self, zo, yo, xo):
        i = self.index(zo, yo, xo)
        src = self.part.at[flat(zo, yo, xo, 1 - self.k)]
        return self.copy(6, i, src, self.chip.at[i], (self.z, self.y, self.x, 1 - self.k))

    def low_y(self, zo):
        i = self.index(zo, 1 - self.y, 1 - self.x)
        src = self.chip.at[i, pl.ds(0, self.low)]
        return self.copy(4, zo, src, self.low_buf.at[zo], (self.z, 1 - self.y, self.x, self.k))

    def high_x(self, zo):
        i = self.index(zo, 1 - self.y, 1 - self.x)
        src = self.chip.at[i, pl.ds(self.low, self.rows - self.low)]
        return self.copy(5, zo, src, self.high_buf.at[zo], (self.z, self.y, 1 - self.x, self.k))

    def to_x(self, zo):
        src = self.chip.at[self.index(zo, self.y, 1 - self.x)]
        return self.copy(2, zo, src, self.x_buf.at[zo], (self.z, self.y, 1 - self.x, self.k))

    def to_y(self, zo):
        src = self.chip.at[self.index(zo, 1 - self.y, self.x)]
        return self.copy(3, zo, src, self.y_buf.at[zo], (self.z, 1 - self.y, self.x, self.k))

    def up(self, zo):
        src = self.chip.at[self.index(zo, self.y, self.x)]
        return self.copy(0, zo, src, self.z_buf.at[zo + 1], (self.z + 1, self.y, self.x, self.k))

    def down(self, zo):
        src = self.chip.at[self.index(zo, self.y, self.x)]
        return self.copy(1, zo, src, self.z_buf.at[zo], (self.z - 1, self.y, self.x, self.k))

    def add(self, i, other, rows=None):
        if rows is None:
            self.chip[i] = self.chip[i] + other
        else:
            self.chip[i, pl.ds(*rows)] = self.chip[i, pl.ds(*rows)] + other

    def each(self, distance, act):
        if distance == 0:
            act(self.z)
        else:
            when(self.z - distance >= 0, lambda: act(self.z - distance))
            when(self.z + distance < self.line, lambda: act(self.z + distance))

    def begin_at(self, zo):
        for yo, xo in ((1 - self.y, 1 - self.x), (self.y, 1 - self.x), (1 - self.y, self.x), (self.y, self.x)):
            self.core(zo, yo, xo).start()

    def begin(self, distance):
        self.each(distance, self.begin_at)

    def corner(self, distance):
        def act(zo):
            for yo, xo in ((1 - self.y, 1 - self.x), (self.y, 1 - self.x), (1 - self.y, self.x), (self.y, self.x)):
                self.core(zo, yo, xo).wait_recv()
                self.add(self.index(zo, yo, xo), self.part[flat(zo, yo, xo, self.k)])
                if yo is not self.y and xo is not self.x:
                    self.low_y(zo).start()
                    if self.low < self.rows:
                        self.high_x(zo).start()

        self.each(distance, act)

    def plane(self, distance):
        def act(zo):
            self.low_y(zo).wait_recv()
            self.add(self.index(zo, self.y, 1 - self.x), self.low_buf[zo], (0, self.low))
            self.to_x(zo).start()
            if self.low < self.rows:
                self.high_x(zo).wait_recv()
                self.add(
                    self.index(zo, 1 - self.y, self.x), self.high_buf[zo], (self.low, self.rows - self.low)
                )
            self.to_y(zo).start()

        self.each(distance, act)

    def along(self, distance):
        own = self.index

        def joined(zo):
            self.to_x(zo).wait_recv()
            self.to_y(zo).wait_recv()
            i = own(zo, self.y, self.x)
            total = self.x_buf[zo].astype(F32) + self.y_buf[zo].astype(F32) + self.chip[i].astype(F32)
            return i, total

        def from_below(zo):
            self.up(zo).wait_recv()
            i = own(zo, self.y, self.x)
            self.add(i, self.z_buf[zo + 1])

        def from_above(zo):
            self.down(zo).wait_recv()
            i = own(zo, self.y, self.x)
            self.add(i, self.z_buf[zo])

        def rising():
            zo = self.z + distance
            i, total = joined(zo)
            self.chip[i] = total.astype(self.chip.dtype)
            when(self.z > 0, lambda: from_below(zo))
            self.up(zo).start()

        def falling():
            zo = self.z - distance
            i, total = joined(zo)
            self.chip[i] = total.astype(self.chip.dtype)
            when(self.z < self.line - 1, lambda: from_above(zo))
            self.down(zo).start()

        if distance:
            when(self.z + distance < self.line, rising)
            when(self.z - distance >= 0, falling)
        else:
            _, total = joined(self.z)
            self.out[...] = total

            def below():
                self.up(self.z).wait_recv()
                self.out[...] += self.z_buf[self.z + 1].astype(F32)

            def above():
                self.down(self.z).wait_recv()
                self.out[...] += self.z_buf[self.z].astype(F32)

            when(self.z > 0, below)
            when(self.z < self.line - 1, above)

    def drain(self):
        for zo in range(self.line):
            when(zo > self.z, lambda: self.up(zo).wait_send())
            when(zo < self.z, lambda: self.down(zo).wait_send())
            self.to_x(zo).wait_send()
            self.to_y(zo).wait_send()
            self.low_y(zo).wait_send()
            if self.low < self.rows:
                self.high_x(zo).wait_send()
            for yo in range(2):
                for xo in range(2):
                    self.core(zo, yo, xo).wait_send()


BUFFERS = 6


def reduce_scratch(line, part):
    _, rows, width = part.shape
    low = low_rows(rows)
    high = max(rows - low, 8)
    sizes = [(line * 4, rows), (line, low), (line, high), (line, rows), (line, rows), (line + 1, rows)]
    return [pltpu.VMEM(s + (width,), part.dtype) for s in sizes]


def dot_rows(a, b, precision=None):
    return lax.dot_general(a, b, (((1,), (1,)), ((), ())), precision=precision, preferred_element_type=F32)


def dot_plain(a, b, precision=None):
    return lax.dot_general(a, b, (((1,), (0,)), ((), ())), precision=precision, preferred_element_type=F32)


def eighths(value):
    return pl.multiple_of(value, 8)


class Exchange:
    def __init__(self, src, dst, sends, recvs, devices):
        self.src, self.dst, self.s, self.r, self.devices = src, dst, sends, recvs, devices
        self.me = flat(*spot())

    def copy(self, i):
        other = lax.rem(self.me + i, self.devices)
        place = (other // 8, other // 4 % 2, other // 2 % 2, other % 2)
        return send(self.src.at[other], self.dst.at[self.me], self.s.at[i], self.r.at[i], place)

    def start(self):
        lax.fori_loop(1, self.devices, lambda i, c: (self.copy(i).start(), c)[1], 0)
        self.dst[self.me] = self.src[self.me]

    def arrive(self):
        lax.fori_loop(1, self.devices, lambda i, c: (self.copy(i).wait_recv(), c)[1], 0)

    def drain(self):
        lax.fori_loop(1, self.devices, lambda i, c: (self.copy(i).wait_send(), c)[1], 0)


def low_lanes(shape):
    return lax.broadcasted_iota(jnp.int32, shape, 1) < 64


def merge_halves(first, second):
    low = low_lanes(first.shape)
    return (
        jnp.where(low, first, pltpu.roll(second, 64, 1)),
        jnp.where(low, pltpu.roll(first, 64, 1), second),
    )


def lane_norm(values, gain, shift):
    center = values - jnp.mean(values, 1, keepdims=True)
    scale_inv = lax.rsqrt(jnp.mean(center * center, 1, keepdims=True) + EPS)
    normal = center * scale_inv
    return normal * gain + shift, normal, scale_inv


def slot_zero(shape):
    return lax.broadcasted_iota(jnp.int32, shape, 1) == 0


def slot_sign(shape):
    return 1.0 - 2.0 * (lax.broadcasted_iota(jnp.int32, shape, 1) % 2).astype(F32)


def slot_weight(shape):
    return jnp.where(slot_zero(shape), 0.5 / shape[1], 1.0 / shape[1])


def column(params, index):
    return params[:, index : index + 1]


def norm_rows(stack, count, chans, width):
    total = None
    for j in range(count):
        tile = stack(j).astype(F32)[:, :128]
        tile = jnp.where(lax.broadcasted_iota(jnp.int32, tile.shape, 1) < chans, tile, 0.0)
        wide = jnp.concatenate([tile, jnp.zeros((tile.shape[0], width - 128), F32)], 1)
        wide = pltpu.roll(wide, j * chans, 1) if j else wide
        total = wide if total is None else total + wide
    return total


RAW = 14


def prepare(in_t, raw, own_in, desk, params, pos_t, mid_t, fil_t, cols):
    gain_one, shift_one, gain_two, shift_two, taps, bias, skip, decay, fil, pos, pos_bias, mid, rate, mid_bias = raw
    chans, order, emb = fil.shape[0], mid.shape[0], pos.shape[0]

    def put(row, values, wide):
        desk[row : row + values.shape[0], :wide] = values.astype(F32)

    desk[...] = jnp.zeros_like(desk)
    for i, ref in enumerate((gain_one, shift_one, gain_two, shift_two)):
        put(i, ref[...], chans)
    norms = jnp.concatenate([desk[:8, :], jnp.zeros((8, in_t.shape[1] - 128), F32)], 1)
    own_in[...] = jnp.concatenate([in_t[...].astype(F32), norms], 0).astype(BF16)
    for i in range(3):
        put(3 * i, taps[i], chans)
    put(9, bias[...], chans)
    put(12, skip[...], chans)
    put(13, decay[...], chans)
    params[...] = desk[...].T[:chans]
    desk[...] = jnp.zeros_like(desk)
    put(0, pos[...], order)
    put(emb, pos_bias[...], order)
    pos_t[...] = desk[...].T[:order, : pos_t.shape[1]]
    desk[...] = jnp.zeros_like(desk)
    put(0, mid[...], order)
    mid_t[...] = desk[...].T[:order, :order]
    desk[...] = jnp.zeros_like(desk)
    put(0, rate[...], order)
    put(1, mid_bias[...], order)
    cols[...] = desk[...].T[:order]
    fil_t[...] = fil[...].astype(F32)


def front_kernel(dims, *refs):
    line, devices, chans, seqs, block, blocks, width = dims
    (in_t, own_out, own_up, own_down, hidden, feats, table) = refs[:7]
    raw = refs[7 : 7 + RAW]
    refs = refs[7 + RAW :]
    (full_in, full_out, full_up, full_down, mixed_in, norms_out, steps, conv, spec, total, k_re, k_alt, k_im) = refs[:13]
    (one, cos_one, two, cos_two, params, pos_t, mid_t, fil_t, cols) = refs[13:22]
    (own_in, desk, proj_send, proj_recv, mix_send, kernel_buf, gated, sums) = refs[22:30]
    (sends, recvs, local, send_a, recv_a, send_b, recv_b) = refs[30:]
    prepare(in_t, raw, own_in, desk, params, pos_t, mid_t, fil_t, cols)
    greet_all(devices)
    pieces = [
        Gather(line, shard, full, sends.at[p], recvs.at[p], local)
        for p, (shard, full) in enumerate(
            ((own_in, full_in), (own_out, full_out), (own_up, full_up), (own_down, full_down))
        )
    ]
    late = (0, 1, 2, 3)

    def tick(now):
        for piece, offset in zip(pieces, late):
            step = now - offset
            if step == 0:
                piece.begin()
            if 1 <= step < line:
                piece.along(step)
            if 1 <= step <= line:
                piece.plane(step - 1)
            if 2 <= step <= line + 1:
                piece.corner(step - 2)

    def filter_part(n, carry):
        sum_one = dot_plain(pos_t[...], feats[n], EXACT)
        phase = column(cols[...], 0) * sum_one
        act_one = jnp.sin(phase)
        one[n] = act_one
        cos_one[n] = jnp.cos(phase)
        phase = column(cols[...], 0) * (dot_plain(mid_t[...], act_one, EXACT) + column(cols[...], 1))
        act_two = jnp.sin(phase)
        two[n] = act_two
        cos_two[n] = jnp.cos(phase)
        lag = lax.broadcasted_iota(jnp.int32, (chans, block), 1) + n * block
        fade = jnp.exp(-lag.astype(F32) * column(params[...], 13))
        kernel_buf[pl.ds(eighths(n * chans), chans), :] = dot_plain(fil_t[...], act_two, EXACT) * fade
        return carry

    def filters(first, last):
        lax.fori_loop(first, last, filter_part, 0)

    def kernel_spectrum():
        ker = dot_plain(kernel_buf[...], table[...], EXACT)
        before = jnp.concatenate([jnp.zeros((chans, 2 * block), F32), ker[:-chans]], 0)
        sign = slot_sign((chans * blocks, block))
        real = ker[:, :block] + sign * before[:, :block]
        imag = ker[:, block:] + sign * before[:, block:]
        zero = slot_zero(real.shape)
        k_re[...] = real
        k_alt[...] = jnp.where(zero, imag, real)
        k_im[...] = jnp.where(zero, 0.0, imag)

    tick(0)
    filters(0, blocks // 4)
    tick(1)
    filters(blocks // 4, blocks // 2)
    tick(2)
    filters(blocks // 2, 3 * blocks // 4)
    tick(3)
    filters(3 * blocks // 4, blocks)
    tick(4)
    kernel_spectrum()
    tick(5)
    pieces[0].finish()

    in_rows = full_in.shape[1]
    norms = norm_rows(lambda j: full_in[j, in_rows - 8 :], devices, chans, width)
    norms_out[...] = norms
    normed, _, _ = lane_norm(hidden[...].astype(F32), norms[0:1], norms[1:2])
    projected = dot_rows(full_in[...].reshape(devices * in_rows, width), normed.astype(BF16))
    projected = projected.reshape(devices, in_rows, 128)
    for j in range(devices):
        for i in range(3):
            unit = 3 * j + i
            proj_send[unit % devices, unit // devices] = projected[j, i * chans : (i + 1) * chans].astype(BF16)
    moved = Exchange(proj_send, proj_recv, send_a, recv_a, devices)
    moved.start()
    tick(6)
    moved.arrive()

    def assemble(j, carry):
        lanes = pl.ds(pl.multiple_of(j * 128, 128), 128)
        for p in range(3):
            pair = merge_halves(proj_recv[2 * j, p].astype(F32), proj_recv[2 * j + 1, p].astype(F32))
            for s in range(seqs):
                steps[p, s, :, lanes] = pair[s]
        return carry

    lax.fori_loop(0, devices // 2, assemble, 0)
    length = block * blocks
    for s in range(seqs):
        for c in range(0, chans, 8):
            spots = lax.broadcasted_iota(jnp.int32, (8, length), 1)
            parts = []
            for p in range(3):
                x = steps[p, s, c : c + 8, :]
                local_params = params[c : c + 8, :]
                value = column(local_params, 9 + p) + column(local_params, p) * x
                for i in (1, 2):
                    value += column(local_params, 3 * i + p) * jnp.where(spots < i, 0.0, pltpu.roll(x, i, 1))
                parts.append(value)
            product = parts[1] * parts[2]
            for n in range(blocks):
                at_rows = (n * seqs + s) * chans + c
                lanes = slice(n * block, (n + 1) * block)
                gated[at_rows : at_rows + 8, :] = product[:, lanes]
                for p in range(3):
                    conv[p, at_rows : at_rows + 8, :] = parts[p][:, lanes]
    tick(7)

    spec[...] = dot_plain(gated[...], table[...], EXACT)
    weight = slot_weight((chans, block))

    def output_block(m, carry):
        def add(n, acc):
            at_kernel = pl.ds(eighths((m - n) * chans), chans)
            kr, ka, ki = k_re[at_kernel, :], k_alt[at_kernel, :], k_im[at_kernel, :]
            result = []
            for s in range(seqs):
                at_signal = pl.ds(eighths((n * seqs + s) * chans), chans)
                re, im = spec[at_signal, :block], spec[at_signal, block:]
                result.append(acc[2 * s] + re * kr - im * ki)
                result.append(acc[2 * s + 1] + re * ki + im * ka)
            return tuple(result)

        acc = lax.fori_loop(0, m + 1, add, tuple(jnp.zeros((chans, block), F32) for _ in range(2 * seqs)))
        for s in range(seqs):
            at_signal = pl.ds(eighths((m * seqs + s) * chans), chans)
            sums[at_signal, :block] = acc[2 * s] * weight
            sums[at_signal, block:] = acc[2 * s + 1] * weight
        return carry

    lax.fori_loop(0, blocks, output_block, 0)
    tick(8)
    total[...] = dot_rows(sums[...], table[...], EXACT)

    def mix(m, carry):
        mixed = []
        for s in range(seqs):
            at_signal = pl.ds(eighths((m * seqs + s) * chans), chans)
            value = total[at_signal, :] + column(params[...], 12) * gated[at_signal, :]
            total[at_signal, :] = value
            mixed.append(value * conv[0, at_signal, :])
        for h in range(block // 128):
            pair = merge_halves(*(v[:, h * 128 : (h + 1) * 128] for v in mixed))
            for q in range(2):
                mix_send[m * (block // 64) + 2 * h + q] = pair[q].astype(BF16)
        return carry

    lax.fori_loop(0, blocks, mix, 0)
    back = Exchange(mix_send, mixed_in, send_b, recv_b, devices)
    back.start()
    for piece in pieces[1:]:
        piece.finish()
    back.arrive()
    for piece in pieces:
        piece.drain()
    moved.drain()
    back.drain()


def front(shards, hidden, feats, table, raw, dims):
    line, devices, chans, seqs, block, blocks, width = dims
    order = raw[-1].shape[1]
    rows = blocks * seqs * chans
    shape = jax.ShapeDtypeStruct
    vmem = pl.BlockSpec(memory_space=pltpu.VMEM)
    in_rows = shards[0].shape[0] + 8
    outs = [shape((devices, s.shape[0] + extra, width), BF16) for s, extra in zip(shards, (8, 0, 0, 0))] + [
        shape((devices, chans, 128), BF16),
        shape((8, width), F32),
        shape((3, seqs, chans, block * blocks), F32),
        shape((3, rows, block), F32),
        shape((rows, 2 * block), F32),
        shape((rows, block), F32),
    ]
    outs += [shape((blocks * chans, block), F32)] * 3 + [shape((blocks, order, block), F32)] * 4
    outs += [shape((chans, 128), F32), shape((order, feats.shape[1]), F32), shape((order, order), F32)]
    outs += [shape((chans, order), F32), shape((order, 128), F32)]
    operands = [*shards, hidden, feats, table, *raw]
    dma = pltpu.SemaphoreType.DMA
    return pl.pallas_call(
        functools.partial(front_kernel, dims),
        name="front",
        out_shape=outs,
        in_specs=[vmem] * len(operands),
        out_specs=[vmem] * len(outs),
        scratch_shapes=[
            pltpu.VMEM((in_rows, width), BF16),
            pltpu.VMEM((128, 128), F32),
            pltpu.VMEM((devices, 3, chans, 128), BF16),
            pltpu.VMEM((devices, 3, chans, 128), BF16),
            pltpu.VMEM((devices, chans, 128), BF16),
            pltpu.VMEM((blocks * chans, block), F32),
            pltpu.VMEM((rows, block), F32),
            pltpu.VMEM((rows, 2 * block), F32),
            dma((4, 7, line * 4)),
            dma((4, 7, line * 4)),
            dma,
            dma((devices,)),
            dma((devices,)),
            dma((devices,)),
            dma((devices,)),
        ],
        compiler_params=pltpu.CompilerParams(collective_id=0, has_side_effects=True, vmem_limit_bytes=KERNEL_VMEM),
    )(*operands)


def lane_norm_back(grad_out, normal, scale_inv, gain):
    grad_normal = grad_out * gain
    inner = grad_normal - jnp.mean(grad_normal, 1, keepdims=True)
    inner = inner - normal * jnp.mean(grad_normal * normal, 1, keepdims=True)
    return inner * scale_inv, jnp.sum(grad_out * normal, 0, keepdims=True), jnp.sum(grad_out, 0, keepdims=True)


def back_kernel(dims, *refs):
    line, devices, chans, seqs, block, blocks, width = dims
    (full_in, full_out, full_up, full_down) = refs[:4]
    (hidden, cot, mixed_in, norms, steps, conv, spec, total, k_re, k_alt, k_im) = refs[4:15]
    (one, cos_one, two, cos_two, params, feats, pos_t, mid_t, fil_t, rows_in, table) = refs[15:26]
    (result, grad_hidden, sum_up, sum_down, sum_out, sum_in, sum_tile, everyone, chan_grads, filter_grad) = refs[26:36]
    (w_in, w_out, w_up, w_down, w_flat, load_sem) = refs[36:42]
    (g_up, g_down, g_out, g_in, g_tile) = refs[42:47]
    (resid, value_sum, second_sum, mix_send, mix_recv, g_long, g_spec, g_sums, g_conv, k_sums) = refs[47:57]
    (proj_send, proj_recv, g_proj, small) = refs[57:61]
    (sends, recvs, share_send, share_recv, local, send_a, recv_a, send_b, recv_b) = refs[61:70]
    buffers = refs[70:]
    shards = full_up.shape[0] // line
    hidden_rows = full_up.shape[1]
    chunk = shards * hidden_rows
    in_rows = full_in.shape[1]

    load_in = pltpu.make_async_copy(full_in, w_in, load_sem.at[0])
    load_out = pltpu.make_async_copy(full_out, w_out, load_sem.at[1])

    def visit(i):
        z = lax.axis_index("blk") // 2
        return lax.rem(z + line // 2 + i, line)

    def load(i):
        slot = i % 2
        source = pl.ds(visit(i) * shards, shards)
        return (
            pltpu.make_async_copy(full_up.at[source], w_up.at[slot], load_sem.at[2 + slot]),
            pltpu.make_async_copy(full_down.at[source], w_down.at[slot], load_sem.at[4 + slot]),
        )

    load_out.start()
    for copy in load(0):
        copy.start()
    load_in.start()
    greet_all(devices)
    parts = (g_up, g_down, g_out, g_in, g_tile)
    outs = (sum_up, sum_down, sum_out, sum_in, sum_tile)
    pieces = [
        Reduce(line, parts[p], outs[p], *buffers[p * BUFFERS : (p + 1) * BUFFERS], sends.at[p], recvs.at[p])
        for p in range(5)
    ]

    def tick(group, step):
        for piece in group:
            if step < line:
                piece.corner(line - 1 - step)
            if 1 <= step <= line:
                piece.plane(line - step)
            if 2 <= step <= line + 1:
                piece.along(line + 1 - step)

    gain_two, shift_two = norms[2:3], norms[3:4]
    mixed = mixed_in[...].astype(F32).reshape(width, 128).T.astype(BF16)
    load_out.wait()
    w_flat[...] = w_out[...].astype(F32).reshape(width, width).astype(BF16)
    resid[...] = hidden[...].astype(F32) + dot_rows(mixed, w_flat[...])
    second, normal_two, inv_two = lane_norm(resid[...], gain_two, shift_two)
    second = second.astype(BF16)
    value_sum[...] = jnp.zeros_like(value_sum)
    second_sum[...] = jnp.zeros_like(second_sum)

    for i in range(line):
        slot = i % 2
        if i + 1 < line:
            for copy in load(i + 1):
                copy.start()
        for copy in load(i):
            copy.wait()
        up = w_up[slot].reshape(chunk, width)
        down = w_down[slot].reshape(chunk, width)
        active, slope = gelu_parts(dot_rows(up, second))
        active = active.astype(BF16)
        grad_upper = (dot_rows(down, cot[...]) * slope).astype(BF16)
        where_to = pl.ds(visit(i) * shards, shards)
        g_down[where_to] = dot_plain(active, cot[...]).astype(BF16).reshape(shards, hidden_rows, width)
        g_up[where_to] = dot_plain(grad_upper, second).astype(BF16).reshape(shards, hidden_rows, width)
        pieces[0].begin_at(visit(i))
        pieces[1].begin_at(visit(i))
        value_sum[...] += dot_plain(active.astype(F32).T.astype(BF16), down)
        second_sum[...] += dot_plain(grad_upper.astype(F32).T.astype(BF16), up)
    result[...] = (resid[...] + value_sum[...]).astype(BF16)
    resid_term, grad_gain_two, grad_shift_two = lane_norm_back(second_sum[...], normal_two, inv_two, gain_two)
    resid[...] = cot[...].astype(F32) + resid_term
    grad_mixed = dot_plain(resid[...].astype(BF16), w_flat[...])
    mix_send[...] = grad_mixed.T.reshape(devices, chans, 128).astype(BF16)
    moved = Exchange(mix_send, mix_recv, send_a, recv_a, devices)
    moved.start()
    grad_branch = resid[...].T.astype(BF16)
    g_out[...] = dot_plain(grad_branch, mixed).reshape(devices, chans, width).astype(BF16)
    for distance in range(line - 1, -1, -1):
        pieces[2].begin(distance)
    first_group = pieces[:3]
    tick(first_group, 0)
    moved.arrive()

    weight = slot_weight((chans, block))
    skip = column(params[...], 12)
    per_block = block // 64

    def arrange(m, carry):
        for h in range(block // 128):
            source = m * per_block + 2 * h
            pair = merge_halves(mix_recv[source].astype(F32), mix_recv[source + 1].astype(F32))
            lanes = slice(h * 128, (h + 1) * 128)
            for s in range(seqs):
                at_rows = pl.ds(eighths((m * seqs + s) * chans), chans)
                place = pl.ds(pl.multiple_of(m * block + h * 128, 128), 128)
                g_conv[0, s, :, place] = pair[s] * total[at_rows, lanes]
                grad = pair[s] * conv[0, at_rows, lanes]
                g_long[at_rows, lanes] = grad
                carry = carry + grad * conv[1, at_rows, lanes] * conv[2, at_rows, lanes]
        return carry

    skip_sum = lax.fori_loop(0, blocks, arrange, jnp.zeros((chans, 128), F32))
    g_spec[...] = dot_plain(g_long[...], table[...], EXACT)
    tick(first_group, 1)

    def signal_block(n, carry):
        def add(m, acc):
            at_kernel = pl.ds(eighths((m - n) * chans), chans)
            kr, ka, ki = k_re[at_kernel, :], k_alt[at_kernel, :], k_im[at_kernel, :]
            out = []
            for s in range(seqs):
                at_rows = pl.ds(eighths((m * seqs + s) * chans), chans)
                re, im = g_spec[at_rows, :block], g_spec[at_rows, block:]
                out.append(acc[2 * s] + re * kr + im * ki)
                out.append(acc[2 * s + 1] + im * ka - re * ki)
            return tuple(out)

        acc = lax.fori_loop(n, blocks, add, tuple(jnp.zeros((chans, block), F32) for _ in range(2 * seqs)))
        for s in range(seqs):
            at_rows = pl.ds(eighths((n * seqs + s) * chans), chans)
            g_sums[at_rows, :block] = acc[2 * s] * weight
            g_sums[at_rows, block:] = acc[2 * s + 1] * weight
        return carry

    lax.fori_loop(0, blocks, signal_block, 0)
    g_sums[:, :block] = dot_rows(g_sums[...], table[...], EXACT)

    def gate_grads(m, carry):
        for s in range(seqs):
            at_rows = pl.ds(eighths((m * seqs + s) * chans), chans)
            place = pl.ds(pl.multiple_of(m * block, block), block)
            grad = g_sums[at_rows, :block] + skip * g_long[at_rows, :]
            g_conv[1, s, :, place] = grad * conv[2, at_rows, :]
            g_conv[2, s, :, place] = grad * conv[1, at_rows, :]
        return carry

    lax.fori_loop(0, blocks, gate_grads, 0)
    tick(first_group, 2)

    length = block * blocks
    for c in range(0, chans, 8):
        col = lax.broadcasted_iota(jnp.int32, (8, 128), 1)
        spots = lax.broadcasted_iota(jnp.int32, (8, length), 1)
        found = jnp.where(col == 12, jnp.sum(skip_sum[c : c + 8], 1, keepdims=True), 0.0)
        local_params = params[c : c + 8, :]
        for p in range(3):
            for s in range(seqs):
                grad = g_conv[p, s, c : c + 8, :]
                x = steps[p, s, c : c + 8, :]
                value = jnp.zeros_like(grad)
                for i in range(3):
                    later = jnp.where(spots < length - i, pltpu.roll(grad, length - i, 1), 0.0) if i else grad
                    value += column(local_params, 3 * i + p) * later
                    found += jnp.where(col == 3 * i + p, jnp.sum(later * x, 1, keepdims=True), 0.0)
                found += jnp.where(col == 9 + p, jnp.sum(grad, 1, keepdims=True), 0.0)
                g_conv[p, s, c : c + 8, :] = value
        chan_grads[c : c + 8, :] = found

    def pack(j, carry):
        lanes = pl.ds(pl.multiple_of(j * 128, 128), 128)
        for p in range(3):
            pair = merge_halves(g_conv[p, 0, :, lanes], g_conv[p, 1, :, lanes])
            proj_send[2 * j, p] = pair[0].astype(BF16)
            proj_send[2 * j + 1, p] = pair[1].astype(BF16)
        return carry

    lax.fori_loop(0, devices // 2, pack, 0)
    home = Exchange(proj_send, proj_recv, send_b, recv_b, devices)
    home.start()
    tick(first_group, 3)

    def kernel_block(d, carry):
        def add(n, acc):
            real, imag = acc
            for s in range(seqs):
                at_signal = pl.ds(eighths((n * seqs + s) * chans), chans)
                at_grad = pl.ds(eighths(((n + d) * seqs + s) * chans), chans)
                s_re, s_im = spec[at_signal, :block], spec[at_signal, block:]
                g_re, g_im = g_spec[at_grad, :block], g_spec[at_grad, block:]
                zero = slot_zero((chans, block))
                same, other = g_re * s_re, g_im * s_im
                real = real + jnp.where(zero, same, same + other)
                imag = imag + jnp.where(zero, other, g_im * s_re - g_re * s_im)
            return real, imag

        empty = jnp.zeros((chans, block), F32)
        real, imag = lax.fori_loop(0, blocks - d, add, (empty, empty))
        at_kernel = pl.ds(eighths(d * chans), chans)
        k_sums[at_kernel, :block] = real
        k_sums[at_kernel, block:] = imag
        return carry

    lax.fori_loop(0, blocks, kernel_block, 0)
    after = jnp.concatenate([k_sums[chans:, :], jnp.zeros((chans, 2 * block), F32)], 0)
    shape = (chans * blocks, block)
    sign, scale = slot_sign(shape), slot_weight(shape)
    k_sums[:, :block] = (k_sums[:, :block] + sign * after[:, :block]) * scale
    k_sums[:, block:] = (k_sums[:, block:] + sign * after[:, block:]) * scale
    k_sums[:, :block] = dot_rows(k_sums[...], table[...], EXACT)
    tick(first_group, 4)

    order = pos_t.shape[0]
    emb = pos_t.shape[1]
    freq = column(rows_in[...], 0)

    def filter_block(n, carry):
        grad_fil, grad_pos, grad_mid, grad_bias = carry
        lag = lax.broadcasted_iota(jnp.int32, (chans, block), 1) + n * block
        fade = jnp.exp(-lag.astype(F32) * column(params[...], 13))
        grad = k_sums[pl.ds(eighths(n * chans), chans), :block] * fade
        grad_fil = grad_fil + dot_rows(grad, two[n], EXACT)
        grad_two = dot_plain(fil_t[...].T, grad, EXACT) * cos_two[n] * freq
        grad_mid = grad_mid + dot_rows(one[n], grad_two, EXACT)
        grad_bias = grad_bias + dot_rows(jnp.ones((8, block), F32), grad_two, EXACT)
        grad_one = dot_plain(mid_t[...].T, grad_two, EXACT) * cos_one[n] * freq
        grad_pos = grad_pos + dot_rows(feats[n], grad_one, EXACT)
        return grad_fil, grad_pos, grad_mid, grad_bias

    zeros = [jnp.zeros(s, F32) for s in ((chans, order), (emb, order), (order, order), (8, order))]
    grad_fil, grad_pos, grad_mid, grad_bias = lax.fori_loop(0, blocks, filter_block, tuple(zeros))
    filter_grad[...] = grad_fil
    rate_bias = rows_in[...].T
    grad_rate = jnp.sum(pos_t[...].T * grad_pos, 0, keepdims=True) + jnp.sum(mid_t[...].T * grad_mid, 0, keepdims=True)
    grad_rate = (grad_rate + rate_bias[1:2] * grad_bias[:1]) / rate_bias[0:1]
    small[...] = jnp.zeros_like(small)
    small[:emb, :order] = grad_pos
    small[emb : emb + order, :order] = grad_mid
    picked = lax.broadcasted_iota(jnp.int32, (8, order), 0)
    small[emb + order : emb + order + 8, :order] = jnp.where(
        picked == 0, grad_bias, jnp.where(picked == 1, grad_rate, 0.0)
    )
    tick(first_group, 5)

    gain_one, shift_one = norms[0:1], norms[1:2]
    normed, normal_one, inv_one = lane_norm(hidden[...].astype(F32), gain_one, shift_one)
    normed = normed.astype(BF16)
    g_proj[...] = jnp.zeros_like(g_proj)
    home.arrive()
    for j in range(devices):
        for i in range(3):
            unit = 3 * j + i
            at_rows = slice(j * in_rows + i * chans, j * in_rows + (i + 1) * chans)
            g_proj[at_rows, :] = proj_recv[unit % devices, unit // devices].astype(F32)
    for i in range(line):
        zo = visit(i)
        group = shards * in_rows
        grads = dot_plain(g_proj[pl.ds(eighths(zo * group), group), :].astype(BF16), normed)
        g_in[pl.ds(zo * shards, shards)] = grads.reshape(shards, in_rows, width)[:, : 3 * chans].astype(BF16)
        pieces[3].begin_at(zo)
    load_in.wait()
    tick(pieces[3:4], 0)
    grad_normed = dot_plain(g_proj[...].T.astype(BF16), w_in[...].reshape(devices * in_rows, width))
    input_term, grad_gain_one, grad_shift_one = lane_norm_back(grad_normed, normal_one, inv_one, gain_one)
    grad_hidden[...] = (resid[...] + input_term).astype(BF16)
    norm_grads = jnp.concatenate(
        [grad_gain_one, grad_shift_one, grad_gain_two, grad_shift_two, jnp.zeros((4, width), F32)], 0
    )
    for j in range(devices):
        turned = pltpu.roll(norm_grads, width - j * chans, 1) if j else norm_grads
        g_tile[j, 0:4, :] = turned[0:4, :128]
        g_tile[j, 4:8, :] = small[4 * j : 4 * j + 4, :]
    for distance in range(line - 1, -1, -1):
        pieces[4].begin(distance)
    tick(pieces[4:5], 0)
    for step in range(1, line + 2):
        tick(pieces[3:], step)

    mine = flat(*spot())

    def share(i):
        other = lax.rem(mine + i, devices)
        place = (other // 8, other // 4 % 2, other // 2 % 2, other % 2)
        return send(sum_tile, everyone.at[mine], share_send.at[i], share_recv.at[i], place)

    keep = pltpu.make_async_copy(sum_tile, everyone.at[mine], local)
    keep.start()
    lax.fori_loop(1, devices, lambda i, c: (share(i).start(), c)[1], 0)
    for piece in pieces:
        piece.drain()
    moved.drain()
    home.drain()
    keep.wait()

    def settle(i, carry):
        share(i).wait_recv()
        share(i).wait_send()
        return carry

    lax.fori_loop(1, devices, settle, 0)


def back(fulls, operands, dims):
    line, devices, chans, seqs, block, blocks, width = dims
    full_in, full_out, full_up, full_down = fulls
    pos_t = operands[17]
    order = pos_t.shape[0]
    rows = blocks * seqs * chans
    shards, hidden_rows = devices // line, full_up.shape[1]
    shape = jax.ShapeDtypeStruct
    vmem = pl.BlockSpec(memory_space=pltpu.VMEM)
    dma = pltpu.SemaphoreType.DMA
    tile = (devices, 8, 128)
    outs = [
        shape((seqs * 64, width), BF16),
        shape((seqs * 64, width), BF16),
        shape((hidden_rows, width), F32),
        shape((hidden_rows, width), F32),
        shape((chans, width), F32),
        shape((3 * chans, width), F32),
        shape(tile[1:], F32),
        shape(tile, F32),
        shape((chans, 128), F32),
        shape((chans, order), F32),
    ]
    parts = [
        shape((devices, hidden_rows, width), BF16),
        shape((devices, hidden_rows, width), BF16),
        shape((devices, chans, width), BF16),
        shape((devices, 3 * chans, width), BF16),
        shape(tile, F32),
    ]
    scratch = [
        pltpu.VMEM(full_in.shape, BF16),
        pltpu.VMEM(full_out.shape, BF16),
        pltpu.VMEM((2, shards, hidden_rows, width), BF16),
        pltpu.VMEM((2, shards, hidden_rows, width), BF16),
        pltpu.VMEM((width, width), BF16),
        dma((6,)),
    ]
    scratch += [pltpu.VMEM(p.shape, p.dtype) for p in parts]
    scratch += [
        pltpu.VMEM((seqs * 64, width), F32),
        pltpu.VMEM((seqs * 64, width), F32),
        pltpu.VMEM((seqs * 64, width), F32),
        pltpu.VMEM((devices, chans, 128), BF16),
        pltpu.VMEM((devices, chans, 128), BF16),
        pltpu.VMEM((rows, block), F32),
        pltpu.VMEM((rows, 2 * block), F32),
        pltpu.VMEM((rows, 2 * block), F32),
        pltpu.VMEM((3, seqs, chans, block * blocks), F32),
        pltpu.VMEM((blocks * chans, 2 * block), F32),
        pltpu.VMEM((devices, 3, chans, 128), BF16),
        pltpu.VMEM((devices, 3, chans, 128), BF16),
        pltpu.VMEM((devices * full_in.shape[1], 128), F32),
        pltpu.VMEM((4 * devices, 128), F32),
    ]
    scratch += [
        dma((5, 7, line * 4)),
        dma((5, 7, line * 4)),
        dma((devices,)),
        dma((devices,)),
        dma,
        dma((devices,)),
        dma((devices,)),
        dma((devices,)),
        dma((devices,)),
    ]
    scratch += [buffer for part in parts for buffer in reduce_scratch(line, part)]
    return pl.pallas_call(
        functools.partial(back_kernel, dims),
        name="back",
        out_shape=outs,
        in_specs=[pl.BlockSpec(memory_space=pl.ANY)] * 4 + [vmem] * len(operands),
        out_specs=[vmem] * len(outs),
        scratch_shapes=scratch,
        compiler_params=pltpu.CompilerParams(collective_id=1, has_side_effects=True, vmem_limit_bytes=KERNEL_VMEM),
    )(*fulls, *operands)


def finish_kernel(emb, order, *refs):
    (result, grad_hidden, up, down, out, inp, tile, everyone, chan_grads, filter_grad) = refs[:10]
    outs, desk = refs[10:-1], refs[-1]
    chans = chan_grads.shape[0]
    for target, source in zip(outs[:7], (result, grad_hidden, up, down, out, inp, filter_grad)):
        target[...] = source[...]
    taps, bias, skip, *gains = outs[7:14]
    desk[...] = jnp.zeros_like(desk)
    desk[:chans, :] = chan_grads[...]
    turned = desk[...].T
    for i in range(3):
        taps[i] = turned[3 * i : 3 * i + 3, :chans]
    bias[...] = turned[9:12, :chans]
    skip[...] = turned[12:13, :chans]
    for i, gain in enumerate(gains):
        gain[...] = tile[i : i + 1, :chans]
    for j in range(everyone.shape[0]):
        desk[4 * j : 4 * j + 4, :] = everyone[j, 4:8, :]
    pos, pos_bias, mid, mid_bias, rate = outs[14:]
    after = emb + 1 + -(emb + 1) % 8
    pos[...] = desk[:emb, :order]
    pos_bias[...] = desk[emb : emb + 1, :order]
    mid[...] = desk[after : after + order, :order]
    mid_bias[...] = desk[after + order : after + order + 1, :order]
    rate[...] = desk[after + order + 1 : after + order + 2, :order]


def finish(parts, pos_shape):
    emb, order = pos_shape
    chans = parts[8].shape[0]
    shape = jax.ShapeDtypeStruct
    vmem = pl.BlockSpec(memory_space=pltpu.VMEM)
    outs = [shape(p.shape, p.dtype) for p in parts[:6]] + [shape(parts[9].shape, F32)]
    outs += [shape((3, 3, chans), F32), shape((3, chans), F32)] + [shape((1, chans), F32)] * 5
    outs += [shape((emb, order), F32), shape((1, order), F32), shape((order, order), F32)]
    outs += [shape((1, order), F32)] * 2
    return pl.pallas_call(
        functools.partial(finish_kernel, emb, order),
        name="finish",
        out_shape=outs,
        in_specs=[vmem] * len(parts),
        out_specs=[vmem] * len(outs),
        scratch_shapes=[pltpu.VMEM((128, 128), F32)],
    )(*parts)


def shards_paired(
    hidden_in,
    cotangent,
    mixer_input_weight,
    mixer_output_weight,
    feedforward_up,
    feedforward_down,
    first_gain,
    first_shift,
    second_gain,
    second_shift,
    short_taps,
    short_bias,
    skip_scale,
    filter_out,
    pos_weight,
    pos_bias,
    mid_weight,
    mid_bias,
    sine_freq,
    decay_rate,
):
    devices = lax.axis_size(AXES)
    micro, seq_count, tok, width = hidden_in.shape
    seqs = micro * seq_count
    tokens = seqs * tok
    length = tok * devices
    chans = width // devices
    block = tok * lax.axis_size("chan")
    blocks = length // block

    line = devices // 8
    def row(vector):
        return vector.reshape(1, -1)

    shards = [mixer_input_weight.T, mixer_output_weight.T, feedforward_up.T, feedforward_down]
    raw = [row(v) for v in (first_gain, first_shift, second_gain, second_shift)]
    raw += [short_taps, short_bias, row(skip_scale), row(decay_rate), filter_out.T]
    raw += [pos_weight, row(pos_bias), mid_weight, row(sine_freq), row(mid_bias)]
    hidden = hidden_in.reshape(tokens, width)
    features, table = jnp.asarray(feature_blocks(length, block)), jnp.asarray(fixed_table(block))
    dims = (line, devices, chans, seqs, block, blocks, width)
    made = front(shards, hidden, features, table, raw, dims)
    fulls, kept, (params, pos_t, mid_t, fil_t, cols) = made[:4], made[4:17], made[17:]
    operands = [hidden, cotangent.reshape(tokens, width), *kept, params, features, pos_t, mid_t, fil_t, cols, table]
    outs = finish(back(fulls, operands, dims), pos_weight.shape)
    result, grad_hidden, up, down, out, inp, filter_grad, taps, bias, skip, *rest = outs
    gains, (pos, pos_bias, mid, mid_bias, rate) = rest[:4], rest[4:]
    return (
        result.reshape(hidden_in.shape),
        grad_hidden.reshape(hidden_in.shape),
        inp.T,
        out.T,
        up.T,
        down,
        *[g.reshape(-1) for g in gains],
        taps,
        bias,
        skip.reshape(-1),
        filter_grad.T,
        pos,
        pos_bias.reshape(-1),
        mid,
        mid_bias.reshape(-1),
        rate.reshape(-1),
    )


def shards(
    hidden_in,
    cotangent,
    mixer_input_weight,
    mixer_output_weight,
    feedforward_up,
    feedforward_down,
    first_gain,
    first_shift,
    second_gain,
    second_shift,
    short_taps,
    short_bias,
    skip_scale,
    filter_out,
    pos_weight,
    pos_bias,
    mid_weight,
    mid_bias,
    sine_freq,
    decay_rate,
):
    devices = lax.axis_size(AXES)
    micro, seq_count, tok, width = hidden_in.shape
    seqs = micro * seq_count
    tokens = seqs * tok
    length = tok * devices
    chans = width // devices
    block = tok * lax.axis_size("chan")
    blocks = length // block

    norms = jnp.stack([first_gain, first_shift, second_gain, second_shift])
    own = [mixer_input_weight.T, feedforward_up.T, feedforward_down, mixer_output_weight.T]
    full = [lax.all_gather(shard, AXES, axis=0, tiled=True) for shard in own]
    norms = lax.all_gather(norms, AXES, axis=1, tiled=True)
    weight_in, weight_up, weight_down, weight_out = full
    norms = norms.astype(F32)
    gain_one, shift_one, gain_two, shift_two = norms[0], norms[1], norms[2], norms[3]

    freq = sine_freq.astype(F32)
    w_pos, w_mid, w_fil = pos_weight.astype(F32), mid_weight.astype(F32), filter_out.astype(F32)
    lags, features, first_sum, first_act, second_sum, second_act = filter_hidden(
        length, w_pos, pos_bias.astype(F32), w_mid, mid_bias.astype(F32), freq
    )
    decay = jnp.exp(-lags[None, :] * decay_rate.astype(F32)[:, None])
    kernel = contract(w_fil, second_act, 0, 0, EXACT) * decay
    table = block_table(block)
    sign = 1.0 - 2.0 * (lax.iota(jnp.int32, block) % 2).astype(F32)
    ker_re, ker_im = to_spectrum(kernel.reshape(chans, blocks, block), table)

    def with_previous(spec):
        before = jnp.concatenate([jnp.zeros_like(spec[:, :1]), spec[:, :-1]], 1)
        return spec + sign * before

    k_re, k_alt, k_im = packed_kernel(with_previous(ker_re), with_previous(ker_im))

    values = hidden_in.reshape(tokens, width).astype(F32)
    normed, normal_one, inv_one = layer_norm(values, gain_one, shift_one)
    normed = normed.astype(BF16)
    projected = contract(weight_in, normed, 1, 1).astype(BF16)
    projected = projected.reshape(3, devices, chans, tokens).transpose(1, 0, 2, 3)
    arrived = exchange(projected)

    def by_sequence(values):
        parts = values.shape[1]
        values = values.reshape(devices, parts, chans, seqs, tok)
        return values.transpose(1, 3, 2, 0, 4).reshape(parts, seqs, chans, length)

    def by_device(values):
        parts = values.shape[0]
        values = values.reshape(parts, seqs, chans, devices, tok)
        return values.transpose(3, 0, 2, 1, 4).reshape(devices, parts, chans, tokens)

    steps = by_sequence(arrived).astype(F32)
    taps = short_taps.astype(F32)[:, :, None, :, None]
    conv = short_bias.astype(F32)[:, None, :, None]
    for i in range(3):
        conv = conv + taps[i] * delayed(steps, i)
    gate_out, gate_in, signal = conv[0], conv[1], conv[2]
    gated = signal * gate_in
    sig_re, sig_im = to_spectrum(gated.reshape(seqs, chans, blocks, block), table)

    def shifted_sum(make):
        total = None
        for d in range(blocks):
            term = make(d)
            total = term if total is None else tuple(a + b for a, b in zip(total, term))
        return total

    def ahead(x, d):
        return x if d == 0 else jnp.pad(x[:, :, :-d], ((0, 0), (0, 0), (d, 0), (0, 0)))

    def back(x, d):
        return x if d == 0 else jnp.pad(x[:, :, d:], ((0, 0), (0, 0), (0, d), (0, 0)))

    def forward_term(d):
        re, im = ahead(sig_re, d), ahead(sig_im, d)
        kr, ka, ki = k_re[:, d : d + 1], k_alt[:, d : d + 1], k_im[:, d : d + 1]
        return re * kr - im * ki, re * ki + im * ka

    out_re, out_im = shifted_sum(forward_term)
    long_out = from_spectrum(out_re, out_im, table).reshape(seqs, chans, length)
    skip = skip_scale.astype(F32)[None, :, None]
    long_total = long_out + skip * gated
    mixed = (long_total * gate_out).astype(BF16)
    mixed = exchange(by_device(mixed[None])).reshape(width, tokens)

    resid = values + contract(mixed, weight_out, 0, 1)
    second, normal_two, inv_two = layer_norm(resid, gain_two, shift_two)
    second = second.astype(BF16)
    upper = contract(second, weight_up, 1, 1)
    active, slope = gelu_parts(upper)
    active = active.astype(BF16)
    result = resid + contract(active, weight_down, 1, 0)

    cot = cotangent.reshape(tokens, width)
    grad_down = contract(active, cot, 0, 0)
    grad_upper = (contract(cot, weight_down, 1, 1) * slope).astype(BF16)
    grad_up = contract(grad_upper, second, 0, 0)
    grad_second = contract(grad_upper, weight_up, 1, 0)
    resid_term, grad_gain_two, grad_shift_two = layer_norm_back(grad_second, normal_two, inv_two, gain_two)
    grad_resid = cot.astype(F32) + resid_term
    grad_branch = grad_resid.astype(BF16)
    grad_out_w = contract(grad_branch, mixed, 0, 1)
    grad_mixed = contract(weight_out, grad_branch, 0, 1).astype(BF16)
    grad_mixed = exchange(grad_mixed.reshape(devices, 1, chans, tokens))
    grad_mixed = by_sequence(grad_mixed)[0].astype(F32)

    grad_gate_out = grad_mixed * long_total
    grad_long = grad_mixed * gate_out
    grad_skip = jnp.sum(grad_long * gated, (0, 2))
    gl_re, gl_im = to_spectrum(grad_long.reshape(seqs, chans, blocks, block), table)

    def signal_term(d):
        re, im = back(gl_re, d), back(gl_im, d)
        kr, ka, ki = k_re[:, d : d + 1], k_alt[:, d : d + 1], k_im[:, d : d + 1]
        return re * kr + im * ki, im * ka - re * ki

    gg_re, gg_im = shifted_sum(signal_term)
    grad_gated = from_spectrum(gg_re, gg_im, table).reshape(seqs, chans, length) + skip * grad_long

    first_slot = lax.iota(jnp.int32, block) == 0
    kg_re, kg_im = [], []
    for d in range(blocks):
        s_re, s_im = sig_re[:, :, : blocks - d], sig_im[:, :, : blocks - d]
        g_re, g_im = gl_re[:, :, d:], gl_im[:, :, d:]
        same, other = g_re * s_re, g_im * s_im
        kg_re.append(jnp.sum(jnp.where(first_slot, same, same + other), (0, 2)))
        kg_im.append(jnp.sum(jnp.where(first_slot, other, g_im * s_re - g_re * s_im), (0, 2)))
    kg_re, kg_im = jnp.stack(kg_re, 1), jnp.stack(kg_im, 1)

    def with_next(spec):
        after = jnp.concatenate([spec[:, 1:], jnp.zeros_like(spec[:, :1])], 1)
        return spec + sign * after

    grad_kernel = from_spectrum(with_next(kg_re), with_next(kg_im), table).reshape(chans, length)

    grad_conv = jnp.stack([grad_gate_out, grad_gated * signal, grad_gated * gate_in])
    grad_bias = jnp.sum(grad_conv, (1, 3))
    grad_taps = jnp.stack([jnp.sum(grad_conv * delayed(steps, i), (1, 3)) for i in range(3)])
    grad_steps = taps[0] * grad_conv
    for i in (1, 2):
        grad_steps = grad_steps + taps[i] * advanced(grad_conv, i)
    grad_proj = exchange(by_device(grad_steps.astype(BF16)))
    grad_proj = grad_proj.transpose(1, 0, 2, 3).reshape(3 * width, tokens)

    fade = grad_kernel * decay
    grad_filter = contract(second_act, fade, 1, 1, EXACT)
    grad_two = contract(w_fil, fade, 1, 0, EXACT) * jnp.cos(freq[:, None] * second_sum)
    grad_freq = jnp.sum(grad_two * second_sum, 1)
    grad_two = grad_two * freq[:, None]
    grad_mid = contract(first_act, grad_two, 1, 1, EXACT)
    grad_one = contract(w_mid, grad_two, 1, 0, EXACT) * jnp.cos(freq[:, None] * first_sum)
    grad_freq = grad_freq + jnp.sum(grad_one * first_sum, 1)
    grad_one = grad_one * freq[:, None]
    grad_pos = contract(features, grad_one, 1, 1, EXACT)
    small = jnp.concatenate(
        [grad_pos, jnp.sum(grad_one, 1)[None], grad_mid, jnp.sum(grad_two, 1)[None], grad_freq[None]]
    )
    emb, order = pos_weight.shape

    grad_in = contract(grad_proj, normed, 1, 0)
    grad_normed = contract(grad_proj, weight_in, 0, 0)
    input_term, grad_gain_one, grad_shift_one = layer_norm_back(grad_normed, normal_one, inv_one, gain_one)
    grad_hidden = (grad_resid + input_term).astype(BF16)

    norm_grads = jnp.stack([grad_gain_one, grad_shift_one, grad_gain_two, grad_shift_two])
    sums = [grad_in, grad_up, grad_down, grad_out_w]
    sums = [
        lax.psum_scatter(g.astype(BF16), AXES, scatter_dimension=0, tiled=True).astype(F32) for g in sums
    ]
    norm_grads = lax.psum_scatter(norm_grads, AXES, scatter_dimension=1, tiled=True)
    small = lax.psum(small, AXES)
    return (
        result.astype(BF16).reshape(hidden_in.shape),
        grad_hidden.reshape(hidden_in.shape),
        sums[0].T,
        sums[3].T,
        sums[1].T,
        sums[2],
        norm_grads[0],
        norm_grads[1],
        norm_grads[2],
        norm_grads[3],
        grad_taps,
        grad_bias,
        grad_skip,
        grad_filter,
        small[:emb],
        small[emb],
        small[emb + 1 : emb + 1 + order],
        small[emb + 1 + order],
        small[emb + 2 + order],
    )


def solution(mesh):
    paired = mesh.shape["chan"] == 4 and mesh.shape["blk"] == 8
    rows, spread, tokens = P(AXES), P(None, AXES), P(None, None, AXES, None)
    params = (rows, rows, rows, rows, P(None, None, AXES), spread, rows, spread, P(), P(), P(), P(), P())
    return jax.shard_map(
        shards_paired if paired else shards,
        mesh=mesh,
        in_specs=(tokens, tokens, spread, spread, spread, P(AXES, None)) + params + (rows,),
        out_specs=(tokens, tokens, spread, spread, spread, P(AXES, None)) + params,
        check_vma=False,
    )
```

profile of v0, /device:TPU:0, one launch (start us, length us, event | category | flops | bytes accessed | tf_op | source)
XLA Modules:
  0.0 226.0 jit_solution(18311361724179918141)
XLA Ops:
  0.7 106.1 %front.1 = (bf16[32,80,768]{2,1,0:T(8,128)(2,1)}, bf16[32,24,768]{2,1,0:T(8,128)(2,1)}, bf16[32,96,768]{2,1,0:T(8,128)(2,1)}, bf16[32,96,768]{2,1,0:T(8,128)(2,1...) custom-call(bf16[72,768]{1,0:T(8,128)(2,1)} %bitcast.37, ...), custom_call_target="tpu_custom_call" | custom-call | tf_op jit(solution)/shard_map/front/pallas_call | solution.py:778
  106.8 116.5 %back.1 = (bf16[128,768]{1,0:T(8,128)(2,1)}, bf16[128,768]{1,0:T(8,128)(2,1)}, f32[96,768]{1,0:T(8,128)}, f32[96,768]{1,0:T(8,128)}, f32[24,768]{1,0:T(8,128)}, ...) custom-call(bf16[32,80,768]{2,1,0:T(8,128)(2,1)} %get-tuple-element.7, ...), custom_call_target="tpu_custom_call" | custom-call | tf_op jit(solution)/shard_map/back/pallas_call | solution.py:1184
  223.3 2.5 %finish.1 = (bf16[128,768]{1,0:T(8,128)(2,1)}, bf16[128,768]{1,0:T(8,128)(2,1)}, f32[96,768]{1,0:T(8,128)}, f32[96,768]{1,0:T(8,128)}, f32[24,768]{1,0:T(8,128)}...) custom-call(bf16[128,768]{1,0:T(8,128)(2,1)} %get-tuple-element.92.r, ...), custom_call_target="tpu_custom_call" | custom-call | tf_op jit(solution)/shard_map/finish/pallas_call | solution.py:1231
where the time goes:
time: 226 us
  Pallas kernels  225 us (100%)
    pallas_call x1, Pallas kernels, back(): pl.pallas_call(functools.partial(back_kernel, dims), name='back', out_sha...  117 us
    pallas_call x1, Pallas kernels, front(): pl.pallas_call(functools.partial(front_kernel, dims), name='front', out_s...  106 us

commit v1 on v0

--- a/solution.py
+++ b/solution.py
@@ -172,23 +172,8 @@
     pl.semaphore_wait(barrier, count - 1)
 
 
-def greet_near(line):
-    z, y, x, k = spot()
-    barrier = pltpu.get_barrier_semaphore()
-
-    def hello(*place):
-        pl.semaphore_signal(barrier, inc=1, device_id=at(*place), device_id_type=MESH)
-
-    hello(z, 1 - y, x, k)
-    hello(z, y, 1 - x, k)
-    hello(z, y, x, 1 - k)
-    when(z > 0, lambda: hello(z - 1, y, x, k))
-    when(z < line - 1, lambda: hello(z + 1, y, x, k))
-    pl.semaphore_wait(barrier, 3 + jnp.minimum(z, 1) + jnp.minimum(line - 1 - z, 1))
-
-
 def low_rows(rows):
-    return max(rows // 16 * 8, 8) if rows > 8 else rows
+    return (rows + 16) // 32 * 16 if rows > 8 else rows
 
 
 class Gather:
@@ -197,6 +182,9 @@
         self.rows = shard.shape[0]
         self.low = low_rows(self.rows)
         self.z, self.y, self.x, self.k = spot()
+        self.half = line // 2
+        self.inward = 1 - 2 * (self.z // self.half)
+        self.inner = self.z == self.half - 1 + self.z // self.half
 
     def copy(self, kind, index, shard, place, rows=None):
         ref = self.full.at[shard] if rows is None else self.full.at[shard, pl.ds(*rows)]
@@ -224,6 +212,13 @@
 
     def core(self, zo, yo, xo, k):
         return self.copy(6, (zo * 2 + yo) * 2 + xo, flat(zo, yo, xo, k), (self.z, self.y, self.x, 1 - self.k))
+
+    def cross(self, zo, step):
+        shard = flat(zo, 1 - self.y, 1 - self.x, self.k)
+        return self.copy(7, zo, shard, (self.z + step, self.y, self.x, self.k))
+
+    def same(self, zo):
+        return zo // self.half == self.z // self.half
 
     def line_has(self, zo):
         self.to_x(zo).start()
@@ -265,20 +260,29 @@
     def plane(self, distance):
         def act(zo):
             self.to_x(zo).wait_recv()
-            self.low_y(zo).start()
+            when(self.same(zo), lambda: self.low_y(zo).start())
             self.core(zo, self.y, 1 - self.x, self.k).start()
             self.to_y(zo).wait_recv()
             if self.low < self.rows:
-                self.high_x(zo).start()
+                when(self.same(zo), lambda: self.high_x(zo).start())
             self.core(zo, 1 - self.y, self.x, self.k).start()
 
         self.each(distance, act)
 
     def corner(self, distance):
-        def act(zo):
+        def near(zo):
             self.low_y(zo, True).wait_recv()
             if self.low < self.rows:
                 self.high_x(zo, True).wait_recv()
+            when(self.inner, lambda: self.cross(zo, self.inward).start())
+
+        def far(zo):
+            self.cross(zo, self.inward).wait_recv()
+            when(self.inner, lambda: self.cross(zo, -self.inward).start())
+
+        def act(zo):
+            when(self.same(zo), lambda: near(zo))
+            when(jnp.logical_not(self.same(zo)), lambda: far(zo))
             self.core(zo, 1 - self.y, 1 - self.x, self.k).start()
 
         self.each(distance, act)
@@ -290,27 +294,35 @@
                     self.core(zo, yo, xo, 1 - self.k).wait_recv()
 
     def drain(self):
+        def near(zo):
+            self.low_y(zo).wait_send()
+            if self.low < self.rows:
+                self.high_x(zo).wait_send()
+
         for zo in range(self.line):
             when(jnp.logical_and(self.z < self.line - 1, zo <= self.z), lambda: self.up(zo).wait_send())
             when(jnp.logical_and(self.z > 0, zo >= self.z), lambda: self.down(zo).wait_send())
             self.to_x(zo).wait_send()
             self.to_y(zo).wait_send()
-            self.low_y(zo).wait_send()
-            if self.low < self.rows:
-                self.high_x(zo).wait_send()
+            when(self.same(zo), lambda: near(zo))
+            when(self.inner, lambda: self.cross(zo, self.inward).wait_send())
             for yo in range(2):
                 for xo in range(2):
                     self.core(zo, yo, xo, self.k).wait_send()
 
 
 class Reduce:
-    def __init__(self, line, part, out, chip, low_y, high_x, by_x, by_y, by_z, sends, recvs):
+    def __init__(self, line, part, out, chip, low_y, high_x, by_x, by_y, by_z, crossed, sends, recvs):
         self.line, self.part, self.out, self.chip = line, part, out, chip
         self.low_buf, self.high_buf, self.x_buf, self.y_buf, self.z_buf = low_y, high_x, by_x, by_y, by_z
+        self.crossed = crossed
         self.s, self.r = sends, recvs
         self.rows = part.shape[1]
         self.low = low_rows(self.rows)
         self.z, self.y, self.x, self.k = spot()
+        self.half = line // 2
+        self.inward = 1 - 2 * (self.z // self.half)
+        self.inner = self.z == self.half - 1 + self.z // self.half
 
     def index(self, zo, yo, xo):
         return (zo * 2 + yo) * 2 + xo
@@ -323,15 +335,16 @@
         src = self.part.at[flat(zo, yo, xo, 1 - self.k)]
         return self.copy(6, i, src, self.chip.at[i], (self.z, self.y, self.x, 1 - self.k))
 
+    def corner_of(self, zo):
+        return self.index(zo, 1 - self.y, 1 - self.x)
+
     def low_y(self, zo):
-        i = self.index(zo, 1 - self.y, 1 - self.x)
-        src = self.chip.at[i, pl.ds(0, self.low)]
-        return self.copy(4, zo, src, self.low_buf.at[zo], (self.z, 1 - self.y, self.x, self.k))
+        src = self.chip.at[self.corner_of(zo), pl.ds(0, self.low)]
+        return self.copy(4, zo, src, self.low_buf.at[zo % self.half], (self.z, 1 - self.y, self.x, self.k))
 
     def high_x(self, zo):
-        i = self.index(zo, 1 - self.y, 1 - self.x)
-        src = self.chip.at[i, pl.ds(self.low, self.rows - self.low)]
-        return self.copy(5, zo, src, self.high_buf.at[zo], (self.z, self.y, 1 - self.x, self.k))
+        src = self.chip.at[self.corner_of(zo), pl.ds(self.low, self.rows - self.low)]
+        return self.copy(5, zo, src, self.high_buf.at[zo % self.half], (self.z, self.y, 1 - self.x, self.k))
 
     def to_x(self, zo):
         src = self.chip.at[self.index(zo, self.y, 1 - self.x)]
@@ -348,6 +361,10 @@
     def down(self, zo):
         src = self.chip.at[self.index(zo, self.y, self.x)]
         return self.copy(1, zo, src, self.z_buf.at[zo], (self.z - 1, self.y, self.x, self.k))
+
+    def cross(self, zo):
+        src = self.chip.at[self.corner_of(zo)]
+        return self.copy(7, zo, src, self.crossed.at[zo], (self.z + self.inward, self.y, self.x, self.k))
 
     def add(self, i, other, rows=None):
         if rows is None:
@@ -355,120 +372,113 @@
         else:
             self.chip[i, pl.ds(*rows)] = self.chip[i, pl.ds(*rows)] + other
 
-    def each(self, distance, act):
-        if distance == 0:
-            act(self.z)
-        else:
-            when(self.z - distance >= 0, lambda: act(self.z - distance))
-            when(self.z + distance < self.line, lambda: act(self.z + distance))
-
-    def begin_at(self, zo):
+    def begin(self, zo):
         for yo, xo in ((1 - self.y, 1 - self.x), (self.y, 1 - self.x), (1 - self.y, self.x), (self.y, self.x)):
             self.core(zo, yo, xo).start()
 
-    def begin(self, distance):
-        self.each(distance, self.begin_at)
-
-    def corner(self, distance):
-        def act(zo):
-            for yo, xo in ((1 - self.y, 1 - self.x), (self.y, 1 - self.x), (1 - self.y, self.x), (self.y, self.x)):
-                self.core(zo, yo, xo).wait_recv()
-                self.add(self.index(zo, yo, xo), self.part[flat(zo, yo, xo, self.k)])
-                if yo is not self.y and xo is not self.x:
-                    self.low_y(zo).start()
-                    if self.low < self.rows:
-                        self.high_x(zo).start()
-
-        self.each(distance, act)
-
-    def plane(self, distance):
-        def act(zo):
-            self.low_y(zo).wait_recv()
-            self.add(self.index(zo, self.y, 1 - self.x), self.low_buf[zo], (0, self.low))
+    def corner(self, zo, near):
+        def joined(yo, xo):
+            self.core(zo, yo, xo).wait_recv()
+            self.add(self.index(zo, yo, xo), self.part[flat(zo, yo, xo, self.k)])
+
+        def crossing():
+            self.cross(zo).wait_recv()
+            self.add(self.corner_of(zo), self.crossed[zo])
+
+        joined(1 - self.y, 1 - self.x)
+        if not near:
+            joined(self.y, 1 - self.x)
             self.to_x(zo).start()
+            joined(1 - self.y, self.x)
+            self.to_y(zo).start()
+        when(self.inner, crossing)
+        if near:
+            self.low_y(zo).start()
             if self.low < self.rows:
-                self.high_x(zo).wait_recv()
-                self.add(
-                    self.index(zo, 1 - self.y, self.x), self.high_buf[zo], (self.low, self.rows - self.low)
-                )
-            self.to_y(zo).start()
-
-        self.each(distance, act)
-
-    def along(self, distance):
-        own = self.index
-
-        def joined(zo):
-            self.to_x(zo).wait_recv()
-            self.to_y(zo).wait_recv()
-            i = own(zo, self.y, self.x)
-            total = self.x_buf[zo].astype(F32) + self.y_buf[zo].astype(F32) + self.chip[i].astype(F32)
-            return i, total
-
-        def from_below(zo):
+                self.high_x(zo).start()
+            joined(self.y, 1 - self.x)
+            joined(1 - self.y, self.x)
+        else:
+            self.cross(zo).start()
+        joined(self.y, self.x)
+
+    def plane(self, zo):
+        self.low_y(zo).wait_recv()
+        self.add(self.index(zo, self.y, 1 - self.x), self.low_buf[zo % self.half], (0, self.low))
+        self.to_x(zo).start()
+        if self.low < self.rows:
+            self.high_x(zo).wait_recv()
+            high = (self.low, self.rows - self.low)
+            self.add(self.index(zo, 1 - self.y, self.x), self.high_buf[zo % self.half], high)
+        self.to_y(zo).start()
+
+    def along(self, zo, own):
+        i = self.index(zo, self.y, self.x)
+        self.to_x(zo).wait_recv()
+        self.to_y(zo).wait_recv()
+        total = self.x_buf[zo].astype(F32) + self.y_buf[zo].astype(F32) + self.chip[i].astype(F32)
+
+        def from_below():
             self.up(zo).wait_recv()
-            i = own(zo, self.y, self.x)
             self.add(i, self.z_buf[zo + 1])
 
-        def from_above(zo):
+        def from_above():
             self.down(zo).wait_recv()
-            i = own(zo, self.y, self.x)
             self.add(i, self.z_buf[zo])
 
         def rising():
-            zo = self.z + distance
-            i, total = joined(zo)
+            when(self.z > 0, from_below)
+            self.up(zo).start()
+
+        def falling():
+            when(self.z < self.line - 1, from_above)
+            self.down(zo).start()
+
+        def last_below():
+            self.up(zo).wait_recv()
+            self.out[...] += self.z_buf[zo + 1].astype(F32)
+
+        def last_above():
+            self.down(zo).wait_recv()
+            self.out[...] += self.z_buf[zo].astype(F32)
+
+        if own:
+            self.out[...] = total
+            when(self.z > 0, last_below)
+            when(self.z < self.line - 1, last_above)
+        else:
             self.chip[i] = total.astype(self.chip.dtype)
-            when(self.z > 0, lambda: from_below(zo))
-            self.up(zo).start()
-
-        def falling():
-            zo = self.z - distance
-            i, total = joined(zo)
-            self.chip[i] = total.astype(self.chip.dtype)
-            when(self.z < self.line - 1, lambda: from_above(zo))
-            self.down(zo).start()
-
-        if distance:
-            when(self.z + distance < self.line, rising)
-            when(self.z - distance >= 0, falling)
-        else:
-            _, total = joined(self.z)
-            self.out[...] = total
-
-            def below():
-                self.up(self.z).wait_recv()
-                self.out[...] += self.z_buf[self.z + 1].astype(F32)
-
-            def above():
-                self.down(self.z).wait_recv()
-                self.out[...] += self.z_buf[self.z].astype(F32)
-
-            when(self.z > 0, below)
-            when(self.z < self.line - 1, above)
+            when(zo > self.z, rising)
+            when(zo < self.z, falling)
 
     def drain(self):
+        def near(zo):
+            self.low_y(zo).wait_send()
+            if self.low < self.rows:
+                self.high_x(zo).wait_send()
+
         for zo in range(self.line):
             when(zo > self.z, lambda: self.up(zo).wait_send())
             when(zo < self.z, lambda: self.down(zo).wait_send())
             self.to_x(zo).wait_send()
             self.to_y(zo).wait_send()
-            self.low_y(zo).wait_send()
-            if self.low < self.rows:
-                self.high_x(zo).wait_send()
+            same = zo // self.half == self.z // self.half
+            when(same, lambda: near(zo))
+            when(jnp.logical_not(same), lambda: self.cross(zo).wait_send())
             for yo in range(2):
                 for xo in range(2):
                     self.core(zo, yo, xo).wait_send()
 
 
-BUFFERS = 6
+BUFFERS = 7
 
 
 def reduce_scratch(line, part):
     _, rows, width = part.shape
     low = low_rows(rows)
     high = max(rows - low, 8)
-    sizes = [(line * 4, rows), (line, low), (line, high), (line, rows), (line, rows), (line + 1, rows)]
+    half = line // 2
+    sizes = [(line * 4, rows), (half, low), (half, high), (line, rows), (line, rows), (line + 1, rows), (line, rows)]
     return [pltpu.VMEM(s + (width,), part.dtype) for s in sizes]
 
 
@@ -586,27 +596,47 @@
     fil_t[...] = fil[...].astype(F32)
 
 
-def front_kernel(dims, *refs):
+def lane_norm_back(grad_out, normal, scale_inv, gain):
+    grad_normal = grad_out * gain
+    inner = grad_normal - jnp.mean(grad_normal, 1, keepdims=True)
+    inner = inner - normal * jnp.mean(grad_normal * normal, 1, keepdims=True)
+    return inner * scale_inv, jnp.sum(grad_out * normal, 0, keepdims=True), jnp.sum(grad_out, 0, keepdims=True)
+
+
+LATE = (0, 2, 3, 4)
+
+
+def layer_kernel(dims, *refs):
     line, devices, chans, seqs, block, blocks, width = dims
-    (in_t, own_out, own_up, own_down, hidden, feats, table) = refs[:7]
-    raw = refs[7 : 7 + RAW]
-    refs = refs[7 + RAW :]
-    (full_in, full_out, full_up, full_down, mixed_in, norms_out, steps, conv, spec, total, k_re, k_alt, k_im) = refs[:13]
+    (in_t, own_out, own_up, own_down, hidden, cot, feats, table) = refs[:8]
+    raw = refs[8 : 8 + RAW]
+    refs = refs[8 + RAW :]
+    (result, grad_hidden, sum_up, sum_down, sum_out, sum_in, sum_tile, everyone, chan_grads, filter_grad) = refs[:10]
+    refs = refs[10:]
+    (full_in, full_out, full_up, full_down, mixed_in, norms_ref, steps, conv, spec, total, k_re, k_alt, k_im) = refs[:13]
     (one, cos_one, two, cos_two, params, pos_t, mid_t, fil_t, cols) = refs[13:22]
     (own_in, desk, proj_send, proj_recv, mix_send, kernel_buf, gated, sums) = refs[22:30]
-    (sends, recvs, local, send_a, recv_a, send_b, recv_b) = refs[30:]
+    (w_flat, g_out, g_in, g_tile, resid, value_sum, second_sum, mix_recv, g_spec, g_conv) = refs[30:40]
+    (k_sums, g_proj, small) = refs[40:43]
+    (gather_send, gather_recv, local, send_a, recv_a, send_b, recv_b, send_c, recv_c, send_d, recv_d) = refs[43:54]
+    (sends, recvs, share_send, share_recv) = refs[54:58]
+    buffers = refs[58:]
+    shards = full_up.shape[0] // line
+    hidden_rows = full_up.shape[1]
+    chunk = shards * hidden_rows
+    gated_grad, g_sums = gated, sums
     prepare(in_t, raw, own_in, desk, params, pos_t, mid_t, fil_t, cols)
     greet_all(devices)
-    pieces = [
-        Gather(line, shard, full, sends.at[p], recvs.at[p], local)
+    gathers = [
+        Gather(line, shard, full, gather_send.at[p], gather_recv.at[p], local)
         for p, (shard, full) in enumerate(
             ((own_in, full_in), (own_out, full_out), (own_up, full_up), (own_down, full_down))
         )
     ]
-    late = (0, 1, 2, 3)
+    late = LATE
 
     def tick(now):
-        for piece, offset in zip(pieces, late):
+        for piece, offset in zip(gathers, late):
             step = now - offset
             if step == 0:
                 piece.begin()
@@ -657,11 +687,11 @@
     tick(4)
     kernel_spectrum()
     tick(5)
-    pieces[0].finish()
+    gathers[0].finish()
 
     in_rows = full_in.shape[1]
     norms = norm_rows(lambda j: full_in[j, in_rows - 8 :], devices, chans, width)
-    norms_out[...] = norms
+    norms_ref[...] = norms
     normed, _, _ = lane_norm(hidden[...].astype(F32), norms[0:1], norms[1:2])
     projected = dot_rows(full_in[...].reshape(devices * in_rows, width), normed.astype(BF16))
     projected = projected.reshape(devices, in_rows, 128)
@@ -744,128 +774,46 @@
         return carry
 
     lax.fori_loop(0, blocks, mix, 0)
-    back = Exchange(mix_send, mixed_in, send_b, recv_b, devices)
-    back.start()
-    for piece in pieces[1:]:
+    mix_home = Exchange(mix_send, mixed_in, send_b, recv_b, devices)
+    mix_home.start()
+    tick(9)
+    for piece in gathers[1:]:
         piece.finish()
-    back.arrive()
-    for piece in pieces:
+    mix_home.arrive()
+    for piece in gathers:
         piece.drain()
     moved.drain()
-    back.drain()
-
-
-def front(shards, hidden, feats, table, raw, dims):
-    line, devices, chans, seqs, block, blocks, width = dims
-    order = raw[-1].shape[1]
-    rows = blocks * seqs * chans
-    shape = jax.ShapeDtypeStruct
-    vmem = pl.BlockSpec(memory_space=pltpu.VMEM)
-    in_rows = shards[0].shape[0] + 8
-    outs = [shape((devices, s.shape[0] + extra, width), BF16) for s, extra in zip(shards, (8, 0, 0, 0))] + [
-        shape((devices, chans, 128), BF16),
-        shape((8, width), F32),
-        shape((3, seqs, chans, block * blocks), F32),
-        shape((3, rows, block), F32),
-        shape((rows, 2 * block), F32),
-        shape((rows, block), F32),
-    ]
-    outs += [shape((blocks * chans, block), F32)] * 3 + [shape((blocks, order, block), F32)] * 4
-    outs += [shape((chans, 128), F32), shape((order, feats.shape[1]), F32), shape((order, order), F32)]
-    outs += [shape((chans, order), F32), shape((order, 128), F32)]
-    operands = [*shards, hidden, feats, table, *raw]
-    dma = pltpu.SemaphoreType.DMA
-    return pl.pallas_call(
-        functools.partial(front_kernel, dims),
-        name="front",
-        out_shape=outs,
-        in_specs=[vmem] * len(operands),
-        out_specs=[vmem] * len(outs),
-        scratch_shapes=[
-            pltpu.VMEM((in_rows, width), BF16),
-            pltpu.VMEM((128, 128), F32),
-            pltpu.VMEM((devices, 3, chans, 128), BF16),
-            pltpu.VMEM((devices, 3, chans, 128), BF16),
-            pltpu.VMEM((devices, chans, 128), BF16),
-            pltpu.VMEM((blocks * chans, block), F32),
-            pltpu.VMEM((rows, block), F32),
-            pltpu.VMEM((rows, 2 * block), F32),
-            dma((4, 7, line * 4)),
-            dma((4, 7, line * 4)),
-            dma,
-            dma((devices,)),
-            dma((devices,)),
-            dma((devices,)),
-            dma((devices,)),
-        ],
-        compiler_params=pltpu.CompilerParams(collective_id=0, has_side_effects=True, vmem_limit_bytes=KERNEL_VMEM),
-    )(*operands)
-
-
-def lane_norm_back(grad_out, normal, scale_inv, gain):
-    grad_normal = grad_out * gain
-    inner = grad_normal - jnp.mean(grad_normal, 1, keepdims=True)
-    inner = inner - normal * jnp.mean(grad_normal * normal, 1, keepdims=True)
-    return inner * scale_inv, jnp.sum(grad_out * normal, 0, keepdims=True), jnp.sum(grad_out, 0, keepdims=True)
-
-
-def back_kernel(dims, *refs):
-    line, devices, chans, seqs, block, blocks, width = dims
-    (full_in, full_out, full_up, full_down) = refs[:4]
-    (hidden, cot, mixed_in, norms, steps, conv, spec, total, k_re, k_alt, k_im) = refs[4:15]
-    (one, cos_one, two, cos_two, params, feats, pos_t, mid_t, fil_t, rows_in, table) = refs[15:26]
-    (result, grad_hidden, sum_up, sum_down, sum_out, sum_in, sum_tile, everyone, chan_grads, filter_grad) = refs[26:36]
-    (w_in, w_out, w_up, w_down, w_flat, load_sem) = refs[36:42]
-    (g_up, g_down, g_out, g_in, g_tile) = refs[42:47]
-    (resid, value_sum, second_sum, mix_send, mix_recv, g_long, g_spec, g_sums, g_conv, k_sums) = refs[47:57]
-    (proj_send, proj_recv, g_proj, small) = refs[57:61]
-    (sends, recvs, share_send, share_recv, local, send_a, recv_a, send_b, recv_b) = refs[61:70]
-    buffers = refs[70:]
-    shards = full_up.shape[0] // line
-    hidden_rows = full_up.shape[1]
-    chunk = shards * hidden_rows
-    in_rows = full_in.shape[1]
-
-    load_in = pltpu.make_async_copy(full_in, w_in, load_sem.at[0])
-    load_out = pltpu.make_async_copy(full_out, w_out, load_sem.at[1])
-
-    def visit(i):
-        z = lax.axis_index("blk") // 2
-        return lax.rem(z + line // 2 + i, line)
-
-    def load(i):
-        slot = i % 2
-        source = pl.ds(visit(i) * shards, shards)
-        return (
-            pltpu.make_async_copy(full_up.at[source], w_up.at[slot], load_sem.at[2 + slot]),
-            pltpu.make_async_copy(full_down.at[source], w_down.at[slot], load_sem.at[4 + slot]),
-        )
-
-    load_out.start()
-    for copy in load(0):
-        copy.start()
-    load_in.start()
-    greet_all(devices)
-    parts = (g_up, g_down, g_out, g_in, g_tile)
+    mix_home.drain()
+
+    parts = (full_up, full_down, g_out, g_in, g_tile)
     outs = (sum_up, sum_down, sum_out, sum_in, sum_tile)
     pieces = [
         Reduce(line, parts[p], outs[p], *buffers[p * BUFFERS : (p + 1) * BUFFERS], sends.at[p], recvs.at[p])
         for p in range(5)
     ]
 
-    def tick(group, step):
+    z = lax.axis_index("blk") // 2
+    half = line // 2
+    flip = z // half
+    mirror = z + flip * (line - 1 - 2 * z)
+
+    def visit(i):
+        near = half - 1 - mirror if i < line - 1 else mirror
+        place = line - 1 - i if i < half else near
+        return place + flip * (line - 1 - 2 * place)
+
+    def fold(group, slot):
         for piece in group:
-            if step < line:
-                piece.corner(line - 1 - step)
-            if 1 <= step <= line:
-                piece.plane(line - step)
-            if 2 <= step <= line + 1:
-                piece.along(line + 1 - step)
-
-    gain_two, shift_two = norms[2:3], norms[3:4]
+            if slot < line:
+                piece.corner(visit(slot), slot >= half)
+            if half < slot <= line:
+                piece.plane(visit(slot - 1))
+            if 2 <= slot <= line + 1:
+                piece.along(visit(slot - 2), slot - 2 == line - 1)
+
+    gain_two, shift_two = norms_ref[2:3], norms_ref[3:4]
     mixed = mixed_in[...].astype(F32).reshape(width, 128).T.astype(BF16)
-    load_out.wait()
-    w_flat[...] = w_out[...].astype(F32).reshape(width, width).astype(BF16)
+    w_flat[...] = full_out[...].astype(F32).reshape(width, width).astype(BF16)
     resid[...] = hidden[...].astype(F32) + dot_rows(mixed, w_flat[...])
     second, normal_two, inv_two = lane_norm(resid[...], gain_two, shift_two)
     second = second.astype(BF16)
@@ -873,38 +821,34 @@
     second_sum[...] = jnp.zeros_like(second_sum)
 
     for i in range(line):
-        slot = i % 2
-        if i + 1 < line:
-            for copy in load(i + 1):
-                copy.start()
-        for copy in load(i):
-            copy.wait()
-        up = w_up[slot].reshape(chunk, width)
-        down = w_down[slot].reshape(chunk, width)
+        where_to = pl.ds(visit(i) * shards, shards)
+        up = full_up[where_to].reshape(chunk, width)
+        down = full_down[where_to].reshape(chunk, width)
         active, slope = gelu_parts(dot_rows(up, second))
         active = active.astype(BF16)
         grad_upper = (dot_rows(down, cot[...]) * slope).astype(BF16)
-        where_to = pl.ds(visit(i) * shards, shards)
-        g_down[where_to] = dot_plain(active, cot[...]).astype(BF16).reshape(shards, hidden_rows, width)
-        g_up[where_to] = dot_plain(grad_upper, second).astype(BF16).reshape(shards, hidden_rows, width)
-        pieces[0].begin_at(visit(i))
-        pieces[1].begin_at(visit(i))
         value_sum[...] += dot_plain(active.astype(F32).T.astype(BF16), down)
         second_sum[...] += dot_plain(grad_upper.astype(F32).T.astype(BF16), up)
+        full_down[where_to] = dot_plain(active, cot[...]).astype(BF16).reshape(shards, hidden_rows, width)
+        full_up[where_to] = dot_plain(grad_upper, second).astype(BF16).reshape(shards, hidden_rows, width)
+        for piece in pieces[:2]:
+            piece.begin(visit(i))
+        if i:
+            fold(pieces[:2], i - 1)
     result[...] = (resid[...] + value_sum[...]).astype(BF16)
     resid_term, grad_gain_two, grad_shift_two = lane_norm_back(second_sum[...], normal_two, inv_two, gain_two)
     resid[...] = cot[...].astype(F32) + resid_term
     grad_mixed = dot_plain(resid[...].astype(BF16), w_flat[...])
     mix_send[...] = grad_mixed.T.reshape(devices, chans, 128).astype(BF16)
-    moved = Exchange(mix_send, mix_recv, send_a, recv_a, devices)
-    moved.start()
+    grad_mix = Exchange(mix_send, mix_recv, send_c, recv_c, devices)
+    grad_mix.start()
     grad_branch = resid[...].T.astype(BF16)
     g_out[...] = dot_plain(grad_branch, mixed).reshape(devices, chans, width).astype(BF16)
-    for distance in range(line - 1, -1, -1):
-        pieces[2].begin(distance)
-    first_group = pieces[:3]
-    tick(first_group, 0)
-    moved.arrive()
+    for i in range(line):
+        pieces[2].begin(visit(i))
+    fold(pieces[:2], line - 1)
+    fold(pieces[2:3], 0)
+    grad_mix.arrive()
 
     weight = slot_weight((chans, block))
     skip = column(params[...], 12)
@@ -920,13 +864,13 @@
                 place = pl.ds(pl.multiple_of(m * block + h * 128, 128), 128)
                 g_conv[0, s, :, place] = pair[s] * total[at_rows, lanes]
                 grad = pair[s] * conv[0, at_rows, lanes]
-                g_long[at_rows, lanes] = grad
+                gated_grad[at_rows, lanes] = grad
                 carry = carry + grad * conv[1, at_rows, lanes] * conv[2, at_rows, lanes]
         return carry
 
     skip_sum = lax.fori_loop(0, blocks, arrange, jnp.zeros((chans, 128), F32))
-    g_spec[...] = dot_plain(g_long[...], table[...], EXACT)
-    tick(first_group, 1)
+    g_spec[...] = dot_plain(gated_grad[...], table[...], EXACT)
+    fold(pieces[2:3], 1)
 
     def signal_block(n, carry):
         def add(m, acc):
@@ -954,13 +898,14 @@
         for s in range(seqs):
             at_rows = pl.ds(eighths((m * seqs + s) * chans), chans)
             place = pl.ds(pl.multiple_of(m * block, block), block)
-            grad = g_sums[at_rows, :block] + skip * g_long[at_rows, :]
+            grad = g_sums[at_rows, :block] + skip * gated_grad[at_rows, :]
             g_conv[1, s, :, place] = grad * conv[2, at_rows, :]
             g_conv[2, s, :, place] = grad * conv[1, at_rows, :]
         return carry
 
     lax.fori_loop(0, blocks, gate_grads, 0)
-    tick(first_group, 2)
+    fold(pieces[:2], line)
+    fold(pieces[2:3], 2)
 
     length = block * blocks
     for c in range(0, chans, 8):
@@ -990,9 +935,10 @@
         return carry
 
     lax.fori_loop(0, devices // 2, pack, 0)
-    home = Exchange(proj_send, proj_recv, send_b, recv_b, devices)
+    home = Exchange(proj_send, proj_recv, send_d, recv_d, devices)
     home.start()
-    tick(first_group, 3)
+    fold(pieces[:2], line + 1)
+    fold(pieces[2:3], 3)
 
     def kernel_block(d, carry):
         def add(n, acc):
@@ -1022,11 +968,11 @@
     k_sums[:, :block] = (k_sums[:, :block] + sign * after[:, :block]) * scale
     k_sums[:, block:] = (k_sums[:, block:] + sign * after[:, block:]) * scale
     k_sums[:, :block] = dot_rows(k_sums[...], table[...], EXACT)
-    tick(first_group, 4)
+    fold(pieces[2:3], 4)
 
     order = pos_t.shape[0]
     emb = pos_t.shape[1]
-    freq = column(rows_in[...], 0)
+    freq = column(cols[...], 0)
 
     def filter_block(n, carry):
         grad_fil, grad_pos, grad_mid, grad_bias = carry
@@ -1044,7 +990,7 @@
     zeros = [jnp.zeros(s, F32) for s in ((chans, order), (emb, order), (order, order), (8, order))]
     grad_fil, grad_pos, grad_mid, grad_bias = lax.fori_loop(0, blocks, filter_block, tuple(zeros))
     filter_grad[...] = grad_fil
-    rate_bias = rows_in[...].T
+    rate_bias = cols[...].T
     grad_rate = jnp.sum(pos_t[...].T * grad_pos, 0, keepdims=True) + jnp.sum(mid_t[...].T * grad_mid, 0, keepdims=True)
     grad_rate = (grad_rate + rate_bias[1:2] * grad_bias[:1]) / rate_bias[0:1]
     small[...] = jnp.zeros_like(small)
@@ -1054,9 +1000,9 @@
     small[emb + order : emb + order + 8, :order] = jnp.where(
         picked == 0, grad_bias, jnp.where(picked == 1, grad_rate, 0.0)
     )
-    tick(first_group, 5)
-
-    gain_one, shift_one = norms[0:1], norms[1:2]
+    fold(pieces[2:3], 5)
+
+    gain_one, shift_one = norms_ref[0:1], norms_ref[1:2]
     normed, normal_one, inv_one = lane_norm(hidden[...].astype(F32), gain_one, shift_one)
     normed = normed.astype(BF16)
     g_proj[...] = jnp.zeros_like(g_proj)
@@ -1071,10 +1017,9 @@
         group = shards * in_rows
         grads = dot_plain(g_proj[pl.ds(eighths(zo * group), group), :].astype(BF16), normed)
         g_in[pl.ds(zo * shards, shards)] = grads.reshape(shards, in_rows, width)[:, : 3 * chans].astype(BF16)
-        pieces[3].begin_at(zo)
-    load_in.wait()
-    tick(pieces[3:4], 0)
-    grad_normed = dot_plain(g_proj[...].T.astype(BF16), w_in[...].reshape(devices * in_rows, width))
+        pieces[3].begin(zo)
+    fold(pieces[3:4], 0)
+    grad_normed = dot_plain(g_proj[...].T.astype(BF16), full_in[...].reshape(devices * in_rows, width))
     input_term, grad_gain_one, grad_shift_one = lane_norm_back(grad_normed, normal_one, inv_one, gain_one)
     grad_hidden[...] = (resid[...] + input_term).astype(BF16)
     norm_grads = jnp.concatenate(
@@ -1084,11 +1029,11 @@
         turned = pltpu.roll(norm_grads, width - j * chans, 1) if j else norm_grads
         g_tile[j, 0:4, :] = turned[0:4, :128]
         g_tile[j, 4:8, :] = small[4 * j : 4 * j + 4, :]
-    for distance in range(line - 1, -1, -1):
-        pieces[4].begin(distance)
-    tick(pieces[4:5], 0)
+    for i in range(line):
+        pieces[4].begin(visit(i))
+    fold(pieces[4:5], 0)
     for step in range(1, line + 2):
-        tick(pieces[3:], step)
+        fold(pieces[3:], step)
 
     mine = flat(*spot())
 
@@ -1102,7 +1047,7 @@
     lax.fori_loop(1, devices, lambda i, c: (share(i).start(), c)[1], 0)
     for piece in pieces:
         piece.drain()
-    moved.drain()
+    grad_mix.drain()
     home.drain()
     keep.wait()
 
@@ -1114,20 +1059,17 @@
     lax.fori_loop(1, devices, settle, 0)
 
 
-def back(fulls, operands, dims):
+def layer(shards, hidden, cot, feats, table, raw, dims):
     line, devices, chans, seqs, block, blocks, width = dims
-    full_in, full_out, full_up, full_down = fulls
-    pos_t = operands[17]
-    order = pos_t.shape[0]
-    rows = blocks * seqs * chans
-    shards, hidden_rows = devices // line, full_up.shape[1]
-    shape = jax.ShapeDtypeStruct
+    order = raw[-1].shape[1]
+    rows, tokens = blocks * seqs * chans, hidden.shape[0]
+    in_rows, hidden_rows = shards[0].shape[0] + 8, shards[2].shape[0]
+    shape, buffer, dma = jax.ShapeDtypeStruct, pltpu.VMEM, pltpu.SemaphoreType.DMA
     vmem = pl.BlockSpec(memory_space=pltpu.VMEM)
-    dma = pltpu.SemaphoreType.DMA
     tile = (devices, 8, 128)
     outs = [
-        shape((seqs * 64, width), BF16),
-        shape((seqs * 64, width), BF16),
+        shape((tokens, width), BF16),
+        shape((tokens, width), BF16),
         shape((hidden_rows, width), F32),
         shape((hidden_rows, width), F32),
         shape((chans, width), F32),
@@ -1137,59 +1079,55 @@
         shape((chans, 128), F32),
         shape((chans, order), F32),
     ]
-    parts = [
-        shape((devices, hidden_rows, width), BF16),
-        shape((devices, hidden_rows, width), BF16),
-        shape((devices, chans, width), BF16),
-        shape((devices, 3 * chans, width), BF16),
-        shape(tile, F32),
+    scratch = [buffer((devices, r, width), BF16) for r in (in_rows, chans, hidden_rows, hidden_rows)]
+    scratch += [
+        buffer((devices, chans, 128), BF16),
+        buffer((8, width), F32),
+        buffer((3, seqs, chans, block * blocks), F32),
+        buffer((3, rows, block), F32),
+        buffer((rows, 2 * block), F32),
+        buffer((rows, block), F32),
     ]
-    scratch = [
-        pltpu.VMEM(full_in.shape, BF16),
-        pltpu.VMEM(full_out.shape, BF16),
-        pltpu.VMEM((2, shards, hidden_rows, width), BF16),
-        pltpu.VMEM((2, shards, hidden_rows, width), BF16),
-        pltpu.VMEM((width, width), BF16),
-        dma((6,)),
+    scratch += [buffer((blocks * chans, block), F32)] * 3 + [buffer((blocks, order, block), F32)] * 4
+    scratch += [buffer((chans, 128), F32), buffer((order, feats.shape[1]), F32), buffer((order, order), F32)]
+    scratch += [buffer((chans, order), F32), buffer((order, 128), F32)]
+    scratch += [
+        buffer((in_rows, width), BF16),
+        buffer((128, 128), F32),
+        buffer((devices, 3, chans, 128), BF16),
+        buffer((devices, 3, chans, 128), BF16),
+        buffer((devices, chans, 128), BF16),
+        buffer((blocks * chans, block), F32),
+        buffer((rows, block), F32),
+        buffer((rows, 2 * block), F32),
+        buffer((width, width), BF16),
+        buffer((devices, chans, width), BF16),
+        buffer((devices, 3 * chans, width), BF16),
+        buffer(tile, F32),
+        buffer((tokens, width), F32),
+        buffer((tokens, width), F32),
+        buffer((tokens, width), F32),
+        buffer((devices, chans, 128), BF16),
+        buffer((rows, 2 * block), F32),
+        buffer((3, seqs, chans, block * blocks), F32),
+        buffer((blocks * chans, 2 * block), F32),
+        buffer((devices * in_rows, 128), F32),
+        buffer((4 * devices, 128), F32),
     ]
-    scratch += [pltpu.VMEM(p.shape, p.dtype) for p in parts]
-    scratch += [
-        pltpu.VMEM((seqs * 64, width), F32),
-        pltpu.VMEM((seqs * 64, width), F32),
-        pltpu.VMEM((seqs * 64, width), F32),
-        pltpu.VMEM((devices, chans, 128), BF16),
-        pltpu.VMEM((devices, chans, 128), BF16),
-        pltpu.VMEM((rows, block), F32),
-        pltpu.VMEM((rows, 2 * block), F32),
-        pltpu.VMEM((rows, 2 * block), F32),
-        pltpu.VMEM((3, seqs, chans, block * blocks), F32),
-        pltpu.VMEM((blocks * chans, 2 * block), F32),
-        pltpu.VMEM((devices, 3, chans, 128), BF16),
-        pltpu.VMEM((devices, 3, chans, 128), BF16),
-        pltpu.VMEM((devices * full_in.shape[1], 128), F32),
-        pltpu.VMEM((4 * devices, 128), F32),
-    ]
-    scratch += [
-        dma((5, 7, line * 4)),
-        dma((5, 7, line * 4)),
-        dma((devices,)),
-        dma((devices,)),
-        dma,
-        dma((devices,)),
-        dma((devices,)),
-        dma((devices,)),
-        dma((devices,)),
-    ]
-    scratch += [buffer for part in parts for buffer in reduce_scratch(line, part)]
+    scratch += [dma((4, 8, line * 4)), dma((4, 8, line * 4)), dma] + [dma((devices,))] * 8
+    scratch += [dma((5, 8, line * 4)), dma((5, 8, line * 4)), dma((devices,)), dma((devices,))]
+    parts = [shape((devices, r, width), BF16) for r in (hidden_rows, hidden_rows, chans, 3 * chans)] + [shape(tile, F32)]
+    scratch += [b for part in parts for b in reduce_scratch(line, part)]
+    operands = [*shards, hidden, cot, feats, table, *raw]
     return pl.pallas_call(
-        functools.partial(back_kernel, dims),
-        name="back",
+        functools.partial(layer_kernel, dims),
+        name="layer",
         out_shape=outs,
-        in_specs=[pl.BlockSpec(memory_space=pl.ANY)] * 4 + [vmem] * len(operands),
+        in_specs=[vmem] * len(operands),
         out_specs=[vmem] * len(outs),
         scratch_shapes=scratch,
-        compiler_params=pltpu.CompilerParams(collective_id=1, has_side_effects=True, vmem_limit_bytes=KERNEL_VMEM),
-    )(*fulls, *operands)
+        compiler_params=pltpu.CompilerParams(collective_id=0, has_side_effects=True, vmem_limit_bytes=KERNEL_VMEM),
+    )(*operands)
 
 
 def finish_kernel(emb, order, *refs):
@@ -1280,10 +1218,8 @@
     hidden = hidden_in.reshape(tokens, width)
     features, table = jnp.asarray(feature_blocks(length, block)), jnp.asarray(fixed_table(block))
     dims = (line, devices, chans, seqs, block, blocks, width)
-    made = front(shards, hidden, features, table, raw, dims)
-    fulls, kept, (params, pos_t, mid_t, fil_t, cols) = made[:4], made[4:17], made[17:]
-    operands = [hidden, cotangent.reshape(tokens, width), *kept, params, features, pos_t, mid_t, fil_t, cols, table]
-    outs = finish(back(fulls, operands, dims), pos_weight.shape)
+    parts = layer(shards, hidden, cotangent.reshape(tokens, width), features, table, raw, dims)
+    outs = finish(parts, pos_weight.shape)
     result, grad_hidden, up, down, out, inp, filter_grad, taps, bias, skip, *rest = outs
     gains, (pos, pos_bias, mid, mid_bias, rate) = rest[:4], rest[4:]
     return (

time: 226 us -> 210 us (0.929)
  Pallas kernels: 225 us -> 209 us
    pallas_call x2 -> x1, Pallas kernels: 223 us -> 207 us  [layer(): pl.pallas_call(functools.partial(layer_kernel, dims), name='layer', out_s...]
where the time goes in v1:
time: 210 us
  Pallas kernels  209 us (100%)
    pallas_call x1, Pallas kernels, layer(): pl.pallas_call(functools.partial(layer_kernel, dims), name='layer', out_s...  207 us

profile of v1, /device:TPU:0, one launch (start us, length us, event | category | flops | bytes accessed | tf_op | source)
XLA Modules:
  0.0 210.3 jit_solution(9685896082446326169)
XLA Ops:
  0.7 206.9 %layer.1 = (bf16[128,768]{1,0:T(8,128)(2,1)}, bf16[128,768]{1,0:T(8,128)(2,1)}, f32[96,768]{1,0:T(8,128)}, f32[96,768]{1,0:T(8,128)}, f32[24,768]{1,0:T(8,128)},...) custom-call(bf16[72,768]{1,0:T(8,128)(2,1)} %bitcast.36, ...), custom_call_target="tpu_custom_call" | custom-call | tf_op jit(solution)/shard_map/layer/pallas_call | solution.py:1122
  207.6 2.5 %finish.1 = (bf16[128,768]{1,0:T(8,128)(2,1)}, bf16[128,768]{1,0:T(8,128)(2,1)}, f32[96,768]{1,0:T(8,128)}, f32[96,768]{1,0:T(8,128)}, f32[24,768]{1,0:T(8,128)}...) custom-call(bf16[128,768]{1,0:T(8,128)(2,1)} %get-tuple-element.48.r, ...), custom_call_target="tpu_custom_call" | custom-call | tf_op jit(solution)/shard_map/finish/pallas_call | solution.py:1169

commit v2 on v1

--- a/solution.py
+++ b/solution.py
@@ -186,36 +186,41 @@
         self.inward = 1 - 2 * (self.z // self.half)
         self.inner = self.z == self.half - 1 + self.z // self.half
 
-    def copy(self, kind, index, shard, place, rows=None):
+    def copy(self, send_at, recv_at, shard, place, rows=None):
         ref = self.full.at[shard] if rows is None else self.full.at[shard, pl.ds(*rows)]
-        return send(ref, ref, self.s.at[kind, index], self.r.at[kind, index], place)
+        return send(ref, ref, self.s.at[send_at], self.r.at[recv_at], place)
+
+    def together(self, send_at, recv_at, count, rows=None):
+        return self.copy(send_at, recv_at, pl.ds(0, count), (self.z, self.y, self.x, 1 - self.k), rows)
 
     def up(self, zo):
-        return self.copy(0, zo, flat(zo, self.y, self.x, self.k), (self.z + 1, self.y, self.x, self.k))
+        return self.copy(zo, zo, flat(zo, self.y, self.x, self.k), (self.z + 1, self.y, self.x, self.k))
 
     def down(self, zo):
-        return self.copy(1, zo, flat(zo, self.y, self.x, self.k), (self.z - 1, self.y, self.x, self.k))
+        return self.copy(self.line + zo, self.line + zo, flat(zo, self.y, self.x, self.k), (self.z - 1, self.y, self.x, self.k))
 
     def to_x(self, zo):
-        return self.copy(2, zo, flat(zo, self.y, self.x, self.k), (self.z, self.y, 1 - self.x, self.k))
+        return self.copy(2 * self.line, 2 * self.line + zo, flat(zo, self.y, self.x, self.k), (self.z, self.y, 1 - self.x, self.k))
 
     def to_y(self, zo):
-        return self.copy(3, zo, flat(zo, self.y, self.x, self.k), (self.z, 1 - self.y, self.x, self.k))
+        return self.copy(2 * self.line + 1, 3 * self.line + zo, flat(zo, self.y, self.x, self.k), (self.z, 1 - self.y, self.x, self.k))
 
     def low_y(self, zo, other_y=False):
         shard = flat(zo, 1 - self.y if other_y else self.y, 1 - self.x, self.k)
-        return self.copy(4, zo, shard, (self.z, 1 - self.y, self.x, self.k), (0, self.low))
+        return self.copy(2 * self.line + 2, 5 * self.line + zo % self.half, shard, (self.z, 1 - self.y, self.x, self.k), (0, self.low))
 
     def high_x(self, zo, other_x=False):
         shard = flat(zo, 1 - self.y, 1 - self.x if other_x else self.x, self.k)
-        return self.copy(5, zo, shard, (self.z, self.y, 1 - self.x, self.k), (self.low, self.rows - self.low))
+        rows = (self.low, self.rows - self.low)
+        recv_at = 5 * self.line + self.half + zo % self.half
+        return self.copy(2 * self.line + 3, recv_at, shard, (self.z, self.y, 1 - self.x, self.k), rows)
 
     def core(self, zo, yo, xo, k):
-        return self.copy(6, (zo * 2 + yo) * 2 + xo, flat(zo, yo, xo, k), (self.z, self.y, self.x, 1 - self.k))
+        return self.copy(2 * self.line + 4, 6 * self.line, flat(zo, yo, xo, k), (self.z, self.y, self.x, 1 - self.k))
 
     def cross(self, zo, step):
         shard = flat(zo, 1 - self.y, 1 - self.x, self.k)
-        return self.copy(7, zo, shard, (self.z + step, self.y, self.x, self.k))
+        return self.copy(2 * self.line + 5, 4 * self.line + zo, shard, (self.z + step, self.y, self.x, self.k))
 
     def same(self, zo):
         return zo // self.half == self.z // self.half
@@ -288,27 +293,20 @@
         self.each(distance, act)
 
     def finish(self):
-        for zo in range(self.line):
-            for yo in range(2):
-                for xo in range(2):
-                    self.core(zo, yo, xo, 1 - self.k).wait_recv()
+        self.together(2 * self.line + 4, 6 * self.line, 4 * self.line).wait_recv()
 
     def drain(self):
-        def near(zo):
-            self.low_y(zo).wait_send()
-            if self.low < self.rows:
-                self.high_x(zo).wait_send()
-
-        for zo in range(self.line):
-            when(jnp.logical_and(self.z < self.line - 1, zo <= self.z), lambda: self.up(zo).wait_send())
+        line, high = self.line, self.rows - self.low
+        for zo in range(line):
+            when(jnp.logical_and(self.z < line - 1, zo <= self.z), lambda: self.up(zo).wait_send())
             when(jnp.logical_and(self.z > 0, zo >= self.z), lambda: self.down(zo).wait_send())
-            self.to_x(zo).wait_send()
-            self.to_y(zo).wait_send()
-            when(self.same(zo), lambda: near(zo))
-            when(self.inner, lambda: self.cross(zo, self.inward).wait_send())
-            for yo in range(2):
-                for xo in range(2):
-                    self.core(zo, yo, xo, self.k).wait_send()
+        self.together(2 * line, 0, line).wait_send()
+        self.together(2 * line + 1, 0, line).wait_send()
+        self.together(2 * line + 2, 0, self.half, (0, self.low)).wait_send()
+        if high:
+            self.together(2 * line + 3, 0, self.half, (self.low, high)).wait_send()
+        self.together(2 * line + 4, 0, 4 * line).wait_send()
+        when(self.inner, lambda: self.together(2 * line + 5, 0, line).wait_send())
 
 
 class Reduce:
@@ -327,44 +325,52 @@
     def index(self, zo, yo, xo):
         return (zo * 2 + yo) * 2 + xo
 
-    def copy(self, kind, index, src, dst, place):
-        return send(src, dst, self.s.at[kind, index], self.r.at[kind, index], place)
+    def copy(self, send_at, recv_at, src, dst, place):
+        return send(src, dst, self.s.at[send_at], self.r.at[recv_at], place)
+
+    def together(self, send_at, recv_at, ref):
+        return self.copy(send_at, recv_at, ref, ref, (self.z, self.y, self.x, 1 - self.k))
 
     def core(self, zo, yo, xo):
         i = self.index(zo, yo, xo)
         src = self.part.at[flat(zo, yo, xo, 1 - self.k)]
-        return self.copy(6, i, src, self.chip.at[i], (self.z, self.y, self.x, 1 - self.k))
+        return self.copy(2 * self.line + 4, 5 * self.line + zo, src, self.chip.at[i], (self.z, self.y, self.x, 1 - self.k))
 
     def corner_of(self, zo):
         return self.index(zo, 1 - self.y, 1 - self.x)
 
     def low_y(self, zo):
         src = self.chip.at[self.corner_of(zo), pl.ds(0, self.low)]
-        return self.copy(4, zo, src, self.low_buf.at[zo % self.half], (self.z, 1 - self.y, self.x, self.k))
+        slot = zo % self.half
+        place = (self.z, 1 - self.y, self.x, self.k)
+        return self.copy(2 * self.line + 2, 6 * self.line + slot, src, self.low_buf.at[slot], place)
 
     def high_x(self, zo):
         src = self.chip.at[self.corner_of(zo), pl.ds(self.low, self.rows - self.low)]
-        return self.copy(5, zo, src, self.high_buf.at[zo % self.half], (self.z, self.y, 1 - self.x, self.k))
+        slot = zo % self.half
+        place = (self.z, self.y, 1 - self.x, self.k)
+        return self.copy(2 * self.line + 3, 6 * self.line + self.half + slot, src, self.high_buf.at[slot], place)
 
     def to_x(self, zo):
         src = self.chip.at[self.index(zo, self.y, 1 - self.x)]
-        return self.copy(2, zo, src, self.x_buf.at[zo], (self.z, self.y, 1 - self.x, self.k))
+        return self.copy(2 * self.line, 2 * self.line + zo, src, self.x_buf.at[zo], (self.z, self.y, 1 - self.x, self.k))
 
     def to_y(self, zo):
         src = self.chip.at[self.index(zo, 1 - self.y, self.x)]
-        return self.copy(3, zo, src, self.y_buf.at[zo], (self.z, 1 - self.y, self.x, self.k))
+        return self.copy(2 * self.line + 1, 3 * self.line + zo, src, self.y_buf.at[zo], (self.z, 1 - self.y, self.x, self.k))
 
     def up(self, zo):
         src = self.chip.at[self.index(zo, self.y, self.x)]
-        return self.copy(0, zo, src, self.z_buf.at[zo + 1], (self.z + 1, self.y, self.x, self.k))
+        return self.copy(zo, zo, src, self.z_buf.at[zo + 1], (self.z + 1, self.y, self.x, self.k))
 
     def down(self, zo):
         src = self.chip.at[self.index(zo, self.y, self.x)]
-        return self.copy(1, zo, src, self.z_buf.at[zo], (self.z - 1, self.y, self.x, self.k))
+        return self.copy(self.line + zo, self.line + zo, src, self.z_buf.at[zo], (self.z - 1, self.y, self.x, self.k))
 
     def cross(self, zo):
         src = self.chip.at[self.corner_of(zo)]
-        return self.copy(7, zo, src, self.crossed.at[zo], (self.z + self.inward, self.y, self.x, self.k))
+        place = (self.z + self.inward, self.y, self.x, self.k)
+        return self.copy(2 * self.line + 5, 4 * self.line + zo, src, self.crossed.at[zo], place)
 
     def add(self, i, other, rows=None):
         if rows is None:
@@ -378,13 +384,14 @@
 
     def corner(self, zo, near):
         def joined(yo, xo):
-            self.core(zo, yo, xo).wait_recv()
             self.add(self.index(zo, yo, xo), self.part[flat(zo, yo, xo, self.k)])
 
         def crossing():
             self.cross(zo).wait_recv()
             self.add(self.corner_of(zo), self.crossed[zo])
 
+        arrived = self.chip.at[pl.ds(4 * zo, 4)]
+        self.together(2 * self.line + 4, 5 * self.line + zo, arrived).wait_recv()
         joined(1 - self.y, 1 - self.x)
         if not near:
             joined(self.y, 1 - self.x)
@@ -452,22 +459,18 @@
             when(zo < self.z, falling)
 
     def drain(self):
-        def near(zo):
-            self.low_y(zo).wait_send()
-            if self.low < self.rows:
-                self.high_x(zo).wait_send()
-
-        for zo in range(self.line):
+        line, low, high = self.line, self.low, self.rows - self.low
+        shards, halves = self.chip.at[pl.ds(0, line)], pl.ds(0, self.half)
+        for zo in range(line):
             when(zo > self.z, lambda: self.up(zo).wait_send())
             when(zo < self.z, lambda: self.down(zo).wait_send())
-            self.to_x(zo).wait_send()
-            self.to_y(zo).wait_send()
-            same = zo // self.half == self.z // self.half
-            when(same, lambda: near(zo))
-            when(jnp.logical_not(same), lambda: self.cross(zo).wait_send())
-            for yo in range(2):
-                for xo in range(2):
-                    self.core(zo, yo, xo).wait_send()
+        self.together(2 * line, 0, shards).wait_send()
+        self.together(2 * line + 1, 0, shards).wait_send()
+        self.together(2 * line + 2, 0, self.chip.at[halves, pl.ds(0, low)]).wait_send()
+        if high:
+            self.together(2 * line + 3, 0, self.chip.at[halves, pl.ds(low, high)]).wait_send()
+        self.together(2 * line + 4, 0, self.part.at[pl.ds(0, 4 * line)]).wait_send()
+        self.together(2 * line + 5, 0, self.chip.at[halves]).wait_send()
 
 
 BUFFERS = 7
@@ -495,24 +498,29 @@
 
 
 class Exchange:
-    def __init__(self, src, dst, sends, recvs, devices):
-        self.src, self.dst, self.s, self.r, self.devices = src, dst, sends, recvs, devices
+    def __init__(self, src, dst, send_sem, recv_sem, devices):
+        self.src, self.dst, self.s, self.r, self.devices = src, dst, send_sem, recv_sem, devices
         self.me = flat(*spot())
 
     def copy(self, i):
         other = lax.rem(self.me + i, self.devices)
         place = (other // 8, other // 4 % 2, other // 2 % 2, other % 2)
-        return send(self.src.at[other], self.dst.at[self.me], self.s.at[i], self.r.at[i], place)
+        return send(self.src.at[other], self.dst.at[self.me], self.s, self.r, place)
+
+    def together(self, ref):
+        z, y, x, k = spot()
+        ref = ref.at[pl.ds(0, self.devices - 1)]
+        return send(ref, ref, self.s, self.r, (z, y, x, 1 - k))
 
     def start(self):
         lax.fori_loop(1, self.devices, lambda i, c: (self.copy(i).start(), c)[1], 0)
         self.dst[self.me] = self.src[self.me]
 
     def arrive(self):
-        lax.fori_loop(1, self.devices, lambda i, c: (self.copy(i).wait_recv(), c)[1], 0)
+        self.together(self.dst).wait_recv()
 
     def drain(self):
-        lax.fori_loop(1, self.devices, lambda i, c: (self.copy(i).wait_send(), c)[1], 0)
+        self.together(self.src).wait_send()
 
 
 def low_lanes(shape):
@@ -618,9 +626,8 @@
     (own_in, desk, proj_send, proj_recv, mix_send, kernel_buf, gated, sums) = refs[22:30]
     (w_flat, g_out, g_in, g_tile, resid, value_sum, second_sum, mix_recv, g_spec, g_conv) = refs[30:40]
     (k_sums, g_proj, small) = refs[40:43]
-    (gather_send, gather_recv, local, send_a, recv_a, send_b, recv_b, send_c, recv_c, send_d, recv_d) = refs[43:54]
-    (sends, recvs, share_send, share_recv) = refs[54:58]
-    buffers = refs[58:]
+    (gather_send, gather_recv, sends, recvs, local, exchange) = refs[43:49]
+    buffers = refs[49:]
     shards = full_up.shape[0] // line
     hidden_rows = full_up.shape[1]
     chunk = shards * hidden_rows
@@ -699,7 +706,7 @@
         for i in range(3):
             unit = 3 * j + i
             proj_send[unit % devices, unit // devices] = projected[j, i * chans : (i + 1) * chans].astype(BF16)
-    moved = Exchange(proj_send, proj_recv, send_a, recv_a, devices)
+    moved = Exchange(proj_send, proj_recv, exchange.at[0], exchange.at[1], devices)
     moved.start()
     tick(6)
     moved.arrive()
@@ -774,7 +781,7 @@
         return carry
 
     lax.fori_loop(0, blocks, mix, 0)
-    mix_home = Exchange(mix_send, mixed_in, send_b, recv_b, devices)
+    mix_home = Exchange(mix_send, mixed_in, exchange.at[2], exchange.at[3], devices)
     mix_home.start()
     tick(9)
     for piece in gathers[1:]:
@@ -840,7 +847,7 @@
     resid[...] = cot[...].astype(F32) + resid_term
     grad_mixed = dot_plain(resid[...].astype(BF16), w_flat[...])
     mix_send[...] = grad_mixed.T.reshape(devices, chans, 128).astype(BF16)
-    grad_mix = Exchange(mix_send, mix_recv, send_c, recv_c, devices)
+    grad_mix = Exchange(mix_send, mix_recv, exchange.at[4], exchange.at[5], devices)
     grad_mix.start()
     grad_branch = resid[...].T.astype(BF16)
     g_out[...] = dot_plain(grad_branch, mixed).reshape(devices, chans, width).astype(BF16)
@@ -935,7 +942,7 @@
         return carry
 
     lax.fori_loop(0, devices // 2, pack, 0)
-    home = Exchange(proj_send, proj_recv, send_d, recv_d, devices)
+    home = Exchange(proj_send, proj_recv, exchange.at[6], exchange.at[7], devices)
     home.start()
     fold(pieces[:2], line + 1)
     fold(pieces[2:3], 3)
@@ -1040,7 +1047,7 @@
     def share(i):
         other = lax.rem(mine + i, devices)
         place = (other // 8, other // 4 % 2, other // 2 % 2, other % 2)
-        return send(sum_tile, everyone.at[mine], share_send.at[i], share_recv.at[i], place)
+        return send(sum_tile, everyone.at[mine], exchange.at[8], exchange.at[9], place)
 
     keep = pltpu.make_async_copy(sum_tile, everyone.at[mine], local)
     keep.start()
@@ -1051,12 +1058,10 @@
     home.drain()
     keep.wait()
 
-    def settle(i, carry):
-        share(i).wait_recv()
-        share(i).wait_send()
-        return carry
-
-    lax.fori_loop(1, devices, settle, 0)
+    arrived = everyone.at[pl.ds(0, devices - 1)]
+    shared = send(arrived, arrived, exchange.at[8], exchange.at[9], (*spot()[:3], 1 - spot()[3]))
+    shared.wait_recv()
+    shared.wait_send()
 
 
 def layer(shards, hidden, cot, feats, table, raw, dims):
@@ -1114,8 +1119,8 @@
         buffer((devices * in_rows, 128), F32),
         buffer((4 * devices, 128), F32),
     ]
-    scratch += [dma((4, 8, line * 4)), dma((4, 8, line * 4)), dma] + [dma((devices,))] * 8
-    scratch += [dma((5, 8, line * 4)), dma((5, 8, line * 4)), dma((devices,)), dma((devices,))]
+    scratch += [dma((4, 2 * line + 6)), dma((4, 6 * line + 1)), dma((5, 2 * line + 6)), dma((5, 7 * line))]
+    scratch += [dma, dma((10,))]
     parts = [shape((devices, r, width), BF16) for r in (hidden_rows, hidden_rows, chans, 3 * chans)] + [shape(tile, F32)]
     scratch += [b for part in parts for b in reduce_scratch(line, part)]
     operands = [*shards, hidden, cot, feats, table, *raw]

time: 210 us -> 190 us (0.905)
  Pallas kernels: 209 us -> 189 us
    pallas_call x1, Pallas kernels: 207 us -> 186 us  [layer(): pl.pallas_call(functools.partial(layer_kernel, dims), name='layer', out_s...]
where the time goes in v2:
time: 190 us
  Pallas kernels  189 us (99%)
    pallas_call x1, Pallas kernels, layer(): pl.pallas_call(functools.partial(layer_kernel, dims), name='layer', out_s...  186 us

profile of v2, /device:TPU:0, one launch (start us, length us, event | category | flops | bytes accessed | tf_op | source)
XLA Modules:
  0.0 189.6 jit_solution(1874935020524156474)
XLA Ops:
  0.7 186.3 %layer.1 = (bf16[128,768]{1,0:T(8,128)(2,1)}, bf16[128,768]{1,0:T(8,128)(2,1)}, f32[96,768]{1,0:T(8,128)}, f32[96,768]{1,0:T(8,128)}, f32[24,768]{1,0:T(8,128)},...) custom-call(bf16[72,768]{1,0:T(8,128)(2,1)} %bitcast.36, ...), custom_call_target="tpu_custom_call" | custom-call | tf_op jit(solution)/shard_map/layer/pallas_call | solution.py:1127
  187.0 2.5 %finish.1 = (bf16[128,768]{1,0:T(8,128)(2,1)}, bf16[128,768]{1,0:T(8,128)(2,1)}, f32[96,768]{1,0:T(8,128)}, f32[96,768]{1,0:T(8,128)}, f32[24,768]{1,0:T(8,128)}...) custom-call(bf16[128,768]{1,0:T(8,128)(2,1)} %get-tuple-element.48.r, ...), custom_call_target="tpu_custom_call" | custom-call | tf_op jit(solution)/shard_map/finish/pallas_call | solution.py:1174

commit v3 on v2

--- a/solution.py
+++ b/solution.py
@@ -155,21 +155,19 @@
     )
 
 
-def greet_all(count):
-    b, c = lax.axis_index("blk"), lax.axis_index("chan")
-    chan = lax.axis_size("chan")
-    me = b * chan + c
+def greet_near(line):
+    z, y, x, k = spot()
     barrier = pltpu.get_barrier_semaphore()
 
-    def one(i, carry):
-        other = lax.rem(me + i, count)
-        pl.semaphore_signal(
-            barrier, inc=1, device_id={"blk": other // chan, "chan": other % chan}, device_id_type=MESH
-        )
-        return carry
-
-    lax.fori_loop(1, count, one, 0)
-    pl.semaphore_wait(barrier, count - 1)
+    def hello(*place):
+        pl.semaphore_signal(barrier, inc=1, device_id=at(*place), device_id_type=MESH)
+
+    hello(z, 1 - y, x, k)
+    hello(z, y, 1 - x, k)
+    hello(z, y, x, 1 - k)
+    when(z > 0, lambda: hello(z - 1, y, x, k))
+    when(z < line - 1, lambda: hello(z + 1, y, x, k))
+    pl.semaphore_wait(barrier, 3 + jnp.minimum(z, 1) + jnp.minimum(line - 1 - z, 1))
 
 
 def low_rows(rows):
@@ -611,7 +609,7 @@
     return inner * scale_inv, jnp.sum(grad_out * normal, 0, keepdims=True), jnp.sum(grad_out, 0, keepdims=True)
 
 
-LATE = (0, 2, 3, 4)
+LATE = (0, 3, 4, 5)
 
 
 def layer_kernel(dims, *refs):
@@ -633,7 +631,7 @@
     chunk = shards * hidden_rows
     gated_grad, g_sums = gated, sums
     prepare(in_t, raw, own_in, desk, params, pos_t, mid_t, fil_t, cols)
-    greet_all(devices)
+    greet_near(line)
     gathers = [
         Gather(line, shard, full, gather_send.at[p], gather_recv.at[p], local)
         for p, (shard, full) in enumerate(
@@ -784,6 +782,7 @@
     mix_home = Exchange(mix_send, mixed_in, exchange.at[2], exchange.at[3], devices)
     mix_home.start()
     tick(9)
+    tick(10)
     for piece in gathers[1:]:
         piece.finish()
     mix_home.arrive()
@@ -840,8 +839,6 @@
         full_up[where_to] = dot_plain(grad_upper, second).astype(BF16).reshape(shards, hidden_rows, width)
         for piece in pieces[:2]:
             piece.begin(visit(i))
-        if i:
-            fold(pieces[:2], i - 1)
     result[...] = (resid[...] + value_sum[...]).astype(BF16)
     resid_term, grad_gain_two, grad_shift_two = lane_norm_back(second_sum[...], normal_two, inv_two, gain_two)
     resid[...] = cot[...].astype(F32) + resid_term
@@ -849,12 +846,11 @@
     mix_send[...] = grad_mixed.T.reshape(devices, chans, 128).astype(BF16)
     grad_mix = Exchange(mix_send, mix_recv, exchange.at[4], exchange.at[5], devices)
     grad_mix.start()
+    fold(pieces[:2], 0)
     grad_branch = resid[...].T.astype(BF16)
     g_out[...] = dot_plain(grad_branch, mixed).reshape(devices, chans, width).astype(BF16)
     for i in range(line):
         pieces[2].begin(visit(i))
-    fold(pieces[:2], line - 1)
-    fold(pieces[2:3], 0)
     grad_mix.arrive()
 
     weight = slot_weight((chans, block))
@@ -877,7 +873,7 @@
 
     skip_sum = lax.fori_loop(0, blocks, arrange, jnp.zeros((chans, 128), F32))
     g_spec[...] = dot_plain(gated_grad[...], table[...], EXACT)
-    fold(pieces[2:3], 1)
+    fold(pieces[:2], 1)
 
     def signal_block(n, carry):
         def add(m, acc):
@@ -911,8 +907,6 @@
         return carry
 
     lax.fori_loop(0, blocks, gate_grads, 0)
-    fold(pieces[:2], line)
-    fold(pieces[2:3], 2)
 
     length = block * blocks
     for c in range(0, chans, 8):
@@ -944,8 +938,7 @@
     lax.fori_loop(0, devices // 2, pack, 0)
     home = Exchange(proj_send, proj_recv, exchange.at[6], exchange.at[7], devices)
     home.start()
-    fold(pieces[:2], line + 1)
-    fold(pieces[2:3], 3)
+    fold(pieces[:2], 2)
 
     def kernel_block(d, carry):
         def add(n, acc):
@@ -975,7 +968,8 @@
     k_sums[:, :block] = (k_sums[:, :block] + sign * after[:, :block]) * scale
     k_sums[:, block:] = (k_sums[:, block:] + sign * after[:, block:]) * scale
     k_sums[:, :block] = dot_rows(k_sums[...], table[...], EXACT)
-    fold(pieces[2:3], 4)
+    fold(pieces[:2], 3)
+    fold(pieces[2:3], 0)
 
     order = pos_t.shape[0]
     emb = pos_t.shape[1]
@@ -1007,7 +1001,8 @@
     small[emb + order : emb + order + 8, :order] = jnp.where(
         picked == 0, grad_bias, jnp.where(picked == 1, grad_rate, 0.0)
     )
-    fold(pieces[2:3], 5)
+    fold(pieces[:2], 4)
+    fold(pieces[2:3], 1)
 
     gain_one, shift_one = norms_ref[0:1], norms_ref[1:2]
     normed, normal_one, inv_one = lane_norm(hidden[...].astype(F32), gain_one, shift_one)
@@ -1026,6 +1021,8 @@
         g_in[pl.ds(zo * shards, shards)] = grads.reshape(shards, in_rows, width)[:, : 3 * chans].astype(BF16)
         pieces[3].begin(zo)
     fold(pieces[3:4], 0)
+    fold(pieces[:2], 5)
+    fold(pieces[2:3], 2)
     grad_normed = dot_plain(g_proj[...].T.astype(BF16), full_in[...].reshape(devices * in_rows, width))
     input_term, grad_gain_one, grad_shift_one = lane_norm_back(grad_normed, normal_one, inv_one, gain_one)
     grad_hidden[...] = (resid[...] + input_term).astype(BF16)
@@ -1039,8 +1036,14 @@
     for i in range(line):
         pieces[4].begin(visit(i))
     fold(pieces[4:5], 0)
-    for step in range(1, line + 2):
-        fold(pieces[3:], step)
+    fold(pieces[3:], 1)
+    fold(pieces[2:3], 3)
+    fold(pieces[3:], 2)
+    fold(pieces[2:3], 4)
+    fold(pieces[3:], 3)
+    fold(pieces[2:3], 5)
+    fold(pieces[3:], 4)
+    fold(pieces[3:], 5)
 
     mine = flat(*spot())
 

time: 190 us -> 181 us (0.953)
  Pallas kernels: 189 us -> 180 us
    pallas_call x1, Pallas kernels: 186 us -> 178 us  [layer(): pl.pallas_call(functools.partial(layer_kernel, dims), name='layer', out_s...]
where the time goes in v3:
time: 181 us
  Pallas kernels  180 us (99%)
    pallas_call x1, Pallas kernels, layer(): pl.pallas_call(functools.partial(layer_kernel, dims), name='layer', out_s...  178 us

profile of v3, /device:TPU:0, one launch (start us, length us, event | category | flops | bytes accessed | tf_op | source)
XLA Modules:
  0.0 181.2 jit_solution(15455863757227612651)
XLA Ops:
  0.7 177.8 %layer.1 = (bf16[128,768]{1,0:T(8,128)(2,1)}, bf16[128,768]{1,0:T(8,128)(2,1)}, f32[96,768]{1,0:T(8,128)}, f32[96,768]{1,0:T(8,128)}, f32[24,768]{1,0:T(8,128)},...) custom-call(bf16[72,768]{1,0:T(8,128)(2,1)} %bitcast.36, ...), custom_call_target="tpu_custom_call" | custom-call | tf_op jit(solution)/shard_map/layer/pallas_call | solution.py:1130
  178.5 2.5 %finish.1 = (bf16[128,768]{1,0:T(8,128)(2,1)}, bf16[128,768]{1,0:T(8,128)(2,1)}, f32[96,768]{1,0:T(8,128)}, f32[96,768]{1,0:T(8,128)}, f32[24,768]{1,0:T(8,128)}...) custom-call(bf16[128,768]{1,0:T(8,128)(2,1)} %get-tuple-element.48.r, ...), custom_call_target="tpu_custom_call" | custom-call | tf_op jit(solution)/shard_map/finish/pallas_call | solution.py:1177

commit v4 on v3

--- a/solution.py
+++ b/solution.py
@@ -623,9 +623,9 @@
     (one, cos_one, two, cos_two, params, pos_t, mid_t, fil_t, cols) = refs[13:22]
     (own_in, desk, proj_send, proj_recv, mix_send, kernel_buf, gated, sums) = refs[22:30]
     (w_flat, g_out, g_in, g_tile, resid, value_sum, second_sum, mix_recv, g_spec, g_conv) = refs[30:40]
-    (k_sums, g_proj, small) = refs[40:43]
-    (gather_send, gather_recv, sends, recvs, local, exchange) = refs[43:49]
-    buffers = refs[49:]
+    (k_sums, g_proj, small, g_rates, sum_rates) = refs[40:45]
+    (gather_send, gather_recv, sends, recvs, local, exchange) = refs[45:51]
+    buffers = refs[51:]
     shards = full_up.shape[0] // line
     hidden_rows = full_up.shape[1]
     chunk = shards * hidden_rows
@@ -791,11 +791,11 @@
     moved.drain()
     mix_home.drain()
 
-    parts = (full_up, full_down, g_out, g_in, g_tile)
-    outs = (sum_up, sum_down, sum_out, sum_in, sum_tile)
+    parts = (full_up, full_down, g_out, g_in, g_tile, g_rates)
+    outs = (sum_up, sum_down, sum_out, sum_in, sum_tile, sum_rates)
     pieces = [
         Reduce(line, parts[p], outs[p], *buffers[p * BUFFERS : (p + 1) * BUFFERS], sends.at[p], recvs.at[p])
-        for p in range(5)
+        for p in range(6)
     ]
 
     z = lax.axis_index("blk") // 2
@@ -1001,8 +1001,14 @@
     small[emb + order : emb + order + 8, :order] = jnp.where(
         picked == 0, grad_bias, jnp.where(picked == 1, grad_rate, 0.0)
     )
+    g_rates[...] = jnp.zeros_like(g_rates)
+    for j in range(devices):
+        g_rates[j, 4:8, :] = small[4 * j : 4 * j + 4, :]
+    for i in range(line):
+        pieces[5].begin(visit(i))
     fold(pieces[:2], 4)
     fold(pieces[2:3], 1)
+    fold(pieces[5:6], 0)
 
     gain_one, shift_one = norms_ref[0:1], norms_ref[1:2]
     normed, normal_one, inv_one = lane_norm(hidden[...].astype(F32), gain_one, shift_one)
@@ -1021,7 +1027,7 @@
         g_in[pl.ds(zo * shards, shards)] = grads.reshape(shards, in_rows, width)[:, : 3 * chans].astype(BF16)
         pieces[3].begin(zo)
     fold(pieces[3:4], 0)
-    fold(pieces[:2], 5)
+    fold(pieces[5:6], 1)
     fold(pieces[2:3], 2)
     grad_normed = dot_plain(g_proj[...].T.astype(BF16), full_in[...].reshape(devices * in_rows, width))
     input_term, grad_gain_one, grad_shift_one = lane_norm_back(grad_normed, normal_one, inv_one, gain_one)
@@ -1032,29 +1038,34 @@
     for j in range(devices):
         turned = pltpu.roll(norm_grads, width - j * chans, 1) if j else norm_grads
         g_tile[j, 0:4, :] = turned[0:4, :128]
-        g_tile[j, 4:8, :] = small[4 * j : 4 * j + 4, :]
+        g_tile[j, 4:8, :] = jnp.zeros((4, 128), F32)
     for i in range(line):
         pieces[4].begin(visit(i))
     fold(pieces[4:5], 0)
-    fold(pieces[3:], 1)
+    fold(pieces[3:5], 1)
     fold(pieces[2:3], 3)
-    fold(pieces[3:], 2)
+    fold(pieces[5:6], 2)
+    fold(pieces[3:5], 2)
     fold(pieces[2:3], 4)
-    fold(pieces[3:], 3)
+    fold(pieces[5:6], 3)
+    fold(pieces[3:5], 3)
+    fold(pieces[:2], 5)
+    fold(pieces[5:6], 4)
     fold(pieces[2:3], 5)
-    fold(pieces[3:], 4)
-    fold(pieces[3:], 5)
-
+    fold(pieces[5:6], 5)
     mine = flat(*spot())
 
     def share(i):
         other = lax.rem(mine + i, devices)
         place = (other // 8, other // 4 % 2, other // 2 % 2, other % 2)
-        return send(sum_tile, everyone.at[mine], exchange.at[8], exchange.at[9], place)
-
-    keep = pltpu.make_async_copy(sum_tile, everyone.at[mine], local)
+        return send(sum_rates, everyone.at[mine], exchange.at[8], exchange.at[9], place)
+
+    keep = pltpu.make_async_copy(sum_rates, everyone.at[mine], local)
     keep.start()
     lax.fori_loop(1, devices, lambda i, c: (share(i).start(), c)[1], 0)
+    fold(pieces[3:5], 4)
+    fold(pieces[3:5], 5)
+
     for piece in pieces:
         piece.drain()
     grad_mix.drain()
@@ -1121,10 +1132,12 @@
         buffer((blocks * chans, 2 * block), F32),
         buffer((devices * in_rows, 128), F32),
         buffer((4 * devices, 128), F32),
+        buffer(tile, F32),
+        buffer(tile[1:], F32),
     ]
-    scratch += [dma((4, 2 * line + 6)), dma((4, 6 * line + 1)), dma((5, 2 * line + 6)), dma((5, 7 * line))]
+    scratch += [dma((4, 2 * line + 6)), dma((4, 6 * line + 1)), dma((6, 2 * line + 6)), dma((6, 7 * line))]
     scratch += [dma, dma((10,))]
-    parts = [shape((devices, r, width), BF16) for r in (hidden_rows, hidden_rows, chans, 3 * chans)] + [shape(tile, F32)]
+    parts = [shape((devices, r, width), BF16) for r in (hidden_rows, hidden_rows, chans, 3 * chans)] + [shape(tile, F32)] * 2
     scratch += [b for part in parts for b in reduce_scratch(line, part)]
     operands = [*shards, hidden, cot, feats, table, *raw]
     return pl.pallas_call(

time: 181 us -> 176 us (0.972)
  Pallas kernels: 180 us -> 175 us
    pallas_call x1, Pallas kernels: 178 us -> 173 us  [layer(): pl.pallas_call(functools.partial(layer_kernel, dims), name='layer', out_s...]
where the time goes in v4:
time: 176 us
  Pallas kernels  175 us (99%)
    pallas_call x1, Pallas kernels, layer(): pl.pallas_call(functools.partial(layer_kernel, dims), name='layer', out_s...  173 us

profile of v4, /device:TPU:0, one launch (start us, length us, event | category | flops | bytes accessed | tf_op | source)
XLA Modules:
  0.0 176.0 jit_solution(14104860125586689071)
XLA Ops:
  0.7 172.6 %layer.1 = (bf16[128,768]{1,0:T(8,128)(2,1)}, bf16[128,768]{1,0:T(8,128)(2,1)}, f32[96,768]{1,0:T(8,128)}, f32[96,768]{1,0:T(8,128)}, f32[24,768]{1,0:T(8,128)},...) custom-call(bf16[72,768]{1,0:T(8,128)(2,1)} %bitcast.36, ...), custom_call_target="tpu_custom_call" | custom-call | tf_op jit(solution)/shard_map/layer/pallas_call | solution.py:1143
  173.3 2.5 %finish.1 = (bf16[128,768]{1,0:T(8,128)(2,1)}, bf16[128,768]{1,0:T(8,128)(2,1)}, f32[96,768]{1,0:T(8,128)}, f32[96,768]{1,0:T(8,128)}, f32[24,768]{1,0:T(8,128)}...) custom-call(bf16[128,768]{1,0:T(8,128)(2,1)} %get-tuple-element.48.r, ...), custom_call_target="tpu_custom_call" | custom-call | tf_op jit(solution)/shard_map/finish/pallas_call | solution.py:1190
